TPU v7x, 32 devices: a whole 2x2x4 slice. The times are simulated.
32 devices in a mesh: dp: 8 (over z, x), tensor: 4 (over y, core).
Axes of the slice: x: 2, y: 2, z: 4, core: 2. Of those that a mesh axis runs over, the one named last changes fastest.
Arguments:
- tokens: bfloat16 [4096, 768], P(('dp', 'tensor')), may hold values from -6 to 6
- place: int32 [8, 512], P('dp'), may hold values from 0 to 511, each once within a row
- lengths: int32 [8, 3], P('dp'), may hold values from 1 to 320, 512 in all within a row
- expert_ids: int32 [2, 4096, 2], P(None, 'dp'), may hold values from 0 to 3, all different within a row
- gate_values: float32 [2, 4096, 2], P(None, 'dp'), may hold values from 0.25 to 1
- cotangent: bfloat16 [4096, 768], P(('dp', 'tensor')), may hold values from -6 to 6
- gain_attn: float32 [2, 768], P(None, 'dp'), may hold values from 0.5 to 1.5
- w_query: float32 [2, 768, 768], P(None, 'dp', 'tensor'), may hold values from -0.21875 to 0.21875
- w_key: float32 [2, 768, 768], P(None, 'dp', 'tensor'), may hold values from -0.21875 to 0.21875
- w_value: float32 [2, 768, 768], P(None, 'dp', 'tensor'), may hold values from -0.21875 to 0.21875
- w_out: float32 [2, 768, 768], P(None, 'tensor', 'dp'), may hold values from -0.75 to 0.75
- gain_ffn: float32 [2, 768], P(None, 'dp'), may hold values from 0.5 to 1.5
- exp_gate: float32 [2, 4, 768, 2048], P(None, None, 'dp', 'tensor'), may hold values from -0.21875 to 0.21875
- exp_up: float32 [2, 4, 768, 2048], P(None, None, 'dp', 'tensor'), may hold values from -0.21875 to 0.21875
- exp_down: float32 [2, 4, 2048, 768], P(None, None, 'tensor', 'dp'), may hold values from -0.1875 to 0.1875
- dense_gate: float32 [2, 768, 2048], P(None, 'dp', 'tensor'), may hold values from -0.21875 to 0.21875
- dense_up: float32 [2, 768, 2048], P(None, 'dp', 'tensor'), may hold values from -0.21875 to 0.21875
- dense_down: float32 [2, 2048, 768], P(None, 'tensor', 'dp'), may hold values from -0.125 to 0.125
Outputs:
- mixed: bfloat16 [4096, 768], P(('dp', 'tensor'))
- input_grad: float32 [4096, 768], P(('dp', 'tensor'))
- grad_gain_attn: float32 [2, 768], P(None, 'dp')
- grad_query: float32 [2, 768, 768], P(None, 'dp', 'tensor')
- grad_key: float32 [2, 768, 768], P(None, 'dp', 'tensor')
- grad_value: float32 [2, 768, 768], P(None, 'dp', 'tensor')
- grad_out: float32 [2, 768, 768], P(None, 'tensor', 'dp')
- grad_gain_ffn: float32 [2, 768], P(None, 'dp')
- grad_exp_gate: float32 [2, 4, 768, 2048], P(None, None, 'dp', 'tensor')
- grad_exp_up: float32 [2, 4, 768, 2048], P(None, None, 'dp', 'tensor')
- grad_exp_down: float32 [2, 4, 2048, 768], P(None, None, 'tensor', 'dp')
- grad_dense_gate: float32 [2, 768, 2048], P(None, 'dp', 'tensor')
- grad_dense_up: float32 [2, 768, 2048], P(None, 'dp', 'tensor')
- grad_dense_down: float32 [2, 2048, 768], P(None, 'tensor', 'dp')
Inputs may be any that keep to these rules, and one draw needn't show every extreme that they name: `place`: each row is a permutation of 0 .. 511. `lengths`: each row sums to 512; its largest entry is exactly 320. `expert_ids`: a token's 2 experts differ; every expert is used by some token of each layer.
All inputs are finite; a program needn't handle non-finite values.
Results may differ from a plain program's by a relative error of at most 0.03.
Values may be sent and summed in bfloat16 or wider, within the bound.
A program may use at most 192 MiB of HBM per device.

v0:
```python
import jax
import jax.numpy as jnp
from jax import lax
from jax.sharding import PartitionSpec as P

HD = 64


EPSILON = 1e-06
MASKED_SCORE = -1e30


def layout(place_row, length_row):
    ends = jnp.cumsum(length_row, dtype=jnp.int32)
    after = place_row[:, None] >= ends[None, :]
    segment = jnp.sum(after.astype(jnp.int32), axis=1, dtype=jnp.int32)
    begins = jnp.sum(jnp.where(after, length_row[None, :], 0), axis=1, dtype=jnp.int32)
    return (segment, place_row - begins)


def rope_tables(position, width):
    half_width = width // 2
    freqs = 10000.0 ** (-jnp.arange(half_width, dtype=jnp.float32) / half_width)
    angles = position.astype(jnp.float32)[:, None] * freqs[None, :]
    return (jnp.cos(angles)[:, None, :], jnp.sin(angles)[:, None, :])


def rotate(values, cosine, sine):
    half_width = values.shape[-1] // 2
    first_half = values[..., :half_width]
    second_half = values[..., half_width:]
    return jnp.concatenate(
        [first_half * cosine - second_half * sine, first_half * sine + second_half * cosine],
        axis=-1,
    )


def unrotate(grads, cosine, sine):
    half_width = grads.shape[-1] // 2
    first_half = grads[..., :half_width]
    second_half = grads[..., half_width:]
    return jnp.concatenate(
        [first_half * cosine + second_half * sine, second_half * cosine - first_half * sine],
        axis=-1,
    )


def normed(values):
    inverse = lax.rsqrt(jnp.mean(values * values, axis=-1, keepdims=True) + EPSILON)
    return (values * inverse, inverse)


def norm_back(grad_normed, gain_row, unit_rows, inverse):
    scaled = grad_normed * gain_row
    return inverse * (scaled - unit_rows * jnp.mean(scaled * unit_rows, axis=-1, keepdims=True))


def combine(id_rows, gate_rows, count):
    slots = (id_rows[:, :, None] == jnp.arange(count, dtype=jnp.int32)[None, None, :]).astype(
        jnp.float32
    )
    return jnp.sum(slots * gate_rows[:, :, None], axis=1)


def silu_parts(values):
    sigma = jax.nn.sigmoid(values)
    return (values * sigma, sigma * (1.0 + values * (1.0 - sigma)))


def gather_normed(rows):
    return lax.all_gather(rows, "tensor", axis=0, tiled=True)


def gather_grads(rows):
    return lax.all_gather(rows, "tensor", axis=0, tiled=True)


def tensor_total(partial_value):
    return lax.psum_scatter(
        partial_value.astype(jnp.bfloat16), "tensor", scatter_dimension=0, tiled=True
    ).astype(jnp.float32)


def tensor_grads(partial_value):
    return lax.psum_scatter(
        partial_value.astype(jnp.bfloat16), "tensor", scatter_dimension=0, tiled=True
    ).astype(jnp.float32)


def gain_total(first, second):
    return lax.psum((first, second), "tensor")


def fetch_weights(shards):
    return (
        lax.all_gather(shards[0], "dp", axis=0, tiled=True),
        lax.all_gather(shards[1], "dp", axis=0, tiled=True),
        lax.all_gather(shards[2], "dp", axis=0, tiled=True),
        lax.all_gather(shards[3], "dp", axis=0, tiled=True),
        lax.all_gather(shards[4], "dp", axis=1, tiled=True),
        lax.all_gather(shards[5], "dp", axis=0, tiled=True),
        lax.all_gather(shards[6], "dp", axis=1, tiled=True),
        lax.all_gather(shards[7], "dp", axis=1, tiled=True),
        lax.all_gather(shards[8], "dp", axis=2, tiled=True),
        lax.all_gather(shards[9], "dp", axis=0, tiled=True),
        lax.all_gather(shards[10], "dp", axis=0, tiled=True),
        lax.all_gather(shards[11], "dp", axis=1, tiled=True),
    )


def fetch_again(shards):
    return (
        lax.all_gather(shards[0], "dp", axis=0, tiled=True),
        lax.all_gather(shards[1], "dp", axis=0, tiled=True),
        lax.all_gather(shards[2], "dp", axis=0, tiled=True),
        lax.all_gather(shards[3], "dp", axis=0, tiled=True),
        lax.all_gather(shards[4], "dp", axis=1, tiled=True),
        lax.all_gather(shards[5], "dp", axis=0, tiled=True),
        lax.all_gather(shards[6], "dp", axis=1, tiled=True),
        lax.all_gather(shards[7], "dp", axis=1, tiled=True),
        lax.all_gather(shards[8], "dp", axis=2, tiled=True),
        lax.all_gather(shards[9], "dp", axis=0, tiled=True),
        lax.all_gather(shards[10], "dp", axis=0, tiled=True),
        lax.all_gather(shards[11], "dp", axis=1, tiled=True),
    )


def sum_layer(grads):
    return (
        lax.psum_scatter(grads[0], "dp", scatter_dimension=0, tiled=True),
        lax.psum_scatter(grads[1], "dp", scatter_dimension=0, tiled=True),
        lax.psum_scatter(grads[2], "dp", scatter_dimension=0, tiled=True),
        lax.psum_scatter(grads[3], "dp", scatter_dimension=0, tiled=True),
        lax.psum_scatter(grads[4], "dp", scatter_dimension=1, tiled=True),
        lax.psum_scatter(grads[5], "dp", scatter_dimension=0, tiled=True),
        lax.psum_scatter(grads[6], "dp", scatter_dimension=1, tiled=True),
        lax.psum_scatter(grads[7], "dp", scatter_dimension=1, tiled=True),
        lax.psum_scatter(grads[8], "dp", scatter_dimension=2, tiled=True),
        lax.psum_scatter(grads[9], "dp", scatter_dimension=0, tiled=True),
        lax.psum_scatter(grads[10], "dp", scatter_dimension=0, tiled=True),
        lax.psum_scatter(grads[11], "dp", scatter_dimension=1, tiled=True),
    )


def attention_scores(query_rot, key_rot, allowed):
    scores = jnp.einsum(
        "qhd,khd->hqk", query_rot, key_rot, preferred_element_type=jnp.float32
    ) * HD ** (-0.5)
    return jnp.where(allowed[None], scores, MASKED_SCORE)


def forward_layer(x_rows, weights, allowed, cosine, sine, id_rows, gate_rows):
    gain_a, w_q, w_k, w_v, w_o, gain_f, e_gate, e_up, e_down, d_gate, d_up, d_down = weights
    heads_here = w_q.shape[1] // HD
    unit_a, inverse_a = normed(x_rows)
    a_in = gather_normed((unit_a * gain_a.astype(jnp.float32)).astype(jnp.bfloat16))
    tok_count = a_in.shape[0]
    query = jnp.dot(a_in, w_q, preferred_element_type=jnp.float32).reshape(
        tok_count, heads_here, HD
    )
    key_raw = jnp.dot(a_in, w_k, preferred_element_type=jnp.float32).reshape(
        tok_count, heads_here, HD
    )
    value = (
        jnp.dot(a_in, w_v, preferred_element_type=jnp.float32)
        .astype(jnp.bfloat16)
        .reshape(tok_count, heads_here, HD)
    )
    query_rot = rotate(query, cosine, sine).astype(jnp.bfloat16)
    key_rot = rotate(key_raw, cosine, sine).astype(jnp.bfloat16)
    scores = attention_scores(query_rot, key_rot, allowed)
    top_score = jnp.max(scores, axis=-1, keepdims=True)
    expo = jnp.exp(scores - top_score)
    total = jnp.sum(expo, axis=-1, keepdims=True)
    probs = (expo / total).astype(jnp.bfloat16)
    log_total = top_score + jnp.log(total)
    attended = (
        jnp.einsum("hqk,khd->qhd", probs, value, preferred_element_type=jnp.float32)
        .astype(jnp.bfloat16)
        .reshape(tok_count, heads_here * HD)
    )
    resid = x_rows + tensor_total(jnp.dot(attended, w_o, preferred_element_type=jnp.float32))
    unit_f, inverse_f = normed(resid)
    b_in = gather_normed((unit_f * gain_f.astype(jnp.float32)).astype(jnp.bfloat16))
    gate_d = jnp.dot(b_in, d_gate, preferred_element_type=jnp.float32)
    up_d = jnp.dot(b_in, d_up, preferred_element_type=jnp.float32)
    hidden_d = (jax.nn.silu(gate_d) * up_d).astype(jnp.bfloat16)
    mixing = jnp.transpose(combine(id_rows, gate_rows, e_gate.shape[0]))[:, :, None]
    gate_e = jnp.einsum("td,edf->etf", b_in, e_gate, preferred_element_type=jnp.float32)
    up_e = jnp.einsum("td,edf->etf", b_in, e_up, preferred_element_type=jnp.float32)
    hidden_e = (mixing * jax.nn.silu(gate_e) * up_e).astype(jnp.bfloat16)
    partial_value = jnp.dot(hidden_d, d_down, preferred_element_type=jnp.float32) + jnp.einsum(
        "etf,efd->td", hidden_e, e_down, preferred_element_type=jnp.float32
    )
    output = resid + tensor_total(partial_value)
    kept = (
        unit_a,
        inverse_a,
        a_in,
        query_rot,
        key_rot,
        value,
        log_total,
        attended,
        unit_f,
        inverse_f,
        b_in,
        gate_d,
        up_d,
        hidden_d,
        mixing,
        gate_e,
        up_e,
        hidden_e,
    )
    return (output, kept)


def backward_layer(grad_y, kept, weights, allowed, cosine, sine):
    gain_a, w_q, w_k, w_v, w_o, gain_f, e_gate, e_up, e_down, d_gate, d_up, d_down = weights
    (
        unit_a,
        inverse_a,
        a_in,
        query_rot,
        key_rot,
        value,
        log_total,
        attended,
        unit_f,
        inverse_f,
        b_in,
        gate_d,
        up_d,
        hidden_d,
        mixing,
        gate_e,
        up_e,
        hidden_e,
    ) = kept
    tok_count = a_in.shape[0]
    heads_here = w_q.shape[1] // HD
    grad_branch = gather_grads(grad_y.astype(jnp.bfloat16))
    grad_d_down = jnp.einsum("tf,td->fd", hidden_d, grad_branch, preferred_element_type=jnp.float32)
    grad_e_down = jnp.einsum(
        "etf,td->efd", hidden_e, grad_branch, preferred_element_type=jnp.float32
    )
    grad_hidden_d = jnp.einsum("td,fd->tf", grad_branch, d_down, preferred_element_type=jnp.float32)
    act_d, slope_d = silu_parts(gate_d)
    grad_gate_d = (grad_hidden_d * up_d * slope_d).astype(jnp.bfloat16)
    grad_up_d = (grad_hidden_d * act_d).astype(jnp.bfloat16)
    grad_hidden_e = (
        jnp.einsum("td,efd->etf", grad_branch, e_down, preferred_element_type=jnp.float32) * mixing
    )
    act_e, slope_e = silu_parts(gate_e)
    grad_gate_e = (grad_hidden_e * up_e * slope_e).astype(jnp.bfloat16)
    grad_up_e = (grad_hidden_e * act_e).astype(jnp.bfloat16)
    grad_d_gate = jnp.einsum("td,tf->df", b_in, grad_gate_d, preferred_element_type=jnp.float32)
    grad_d_up = jnp.einsum("td,tf->df", b_in, grad_up_d, preferred_element_type=jnp.float32)
    grad_e_gate = jnp.einsum("td,etf->edf", b_in, grad_gate_e, preferred_element_type=jnp.float32)
    grad_e_up = jnp.einsum("td,etf->edf", b_in, grad_up_e, preferred_element_type=jnp.float32)
    partial_b = jnp.einsum("tf,df->td", grad_gate_d, d_gate, preferred_element_type=jnp.float32)
    partial_b = partial_b + jnp.einsum(
        "tf,df->td", grad_up_d, d_up, preferred_element_type=jnp.float32
    )
    partial_b = partial_b + jnp.einsum(
        "etf,edf->td", grad_gate_e, e_gate, preferred_element_type=jnp.float32
    )
    partial_b = partial_b + jnp.einsum(
        "etf,edf->td", grad_up_e, e_up, preferred_element_type=jnp.float32
    )
    grad_b = tensor_grads(partial_b)
    part_gain_f = jnp.sum(grad_b * unit_f, axis=0)
    grad_resid = grad_y + norm_back(grad_b, gain_f.astype(jnp.float32), unit_f, inverse_f)
    grad_attn = gather_grads(grad_resid.astype(jnp.bfloat16))
    grad_w_out = jnp.einsum("tc,td->cd", attended, grad_attn, preferred_element_type=jnp.float32)
    grad_attended = (
        jnp.einsum("td,cd->tc", grad_attn, w_o, preferred_element_type=jnp.float32)
        .astype(jnp.bfloat16)
        .reshape(tok_count, heads_here, HD)
    )
    scores = attention_scores(query_rot, key_rot, allowed)
    probs_full = jnp.exp(scores - log_total)
    probs = probs_full.astype(jnp.bfloat16)
    grad_value = (
        jnp.einsum("hqk,qhd->khd", probs, grad_attended, preferred_element_type=jnp.float32)
        .astype(jnp.bfloat16)
        .reshape(tok_count, heads_here * HD)
    )
    grad_probs = jnp.einsum(
        "qhd,khd->hqk", grad_attended, value, preferred_element_type=jnp.float32
    )
    grad_scores = (
        probs_full * (grad_probs - jnp.sum(grad_probs * probs_full, axis=-1, keepdims=True))
    ).astype(jnp.bfloat16)
    grad_qrot = jnp.einsum(
        "hqk,khd->qhd", grad_scores, key_rot, preferred_element_type=jnp.float32
    ) * HD ** (-0.5)
    grad_krot = jnp.einsum(
        "hqk,qhd->khd", grad_scores, query_rot, preferred_element_type=jnp.float32
    ) * HD ** (-0.5)
    grad_query_raw = (
        unrotate(grad_qrot, cosine, sine).astype(jnp.bfloat16).reshape(tok_count, heads_here * HD)
    )
    grad_key_raw = (
        unrotate(grad_krot, cosine, sine).astype(jnp.bfloat16).reshape(tok_count, heads_here * HD)
    )
    grad_w_q = jnp.einsum("td,tc->dc", a_in, grad_query_raw, preferred_element_type=jnp.float32)
    grad_w_k = jnp.einsum("td,tc->dc", a_in, grad_key_raw, preferred_element_type=jnp.float32)
    grad_w_v = jnp.einsum("td,tc->dc", a_in, grad_value, preferred_element_type=jnp.float32)
    partial_a = jnp.einsum("tc,dc->td", grad_query_raw, w_q, preferred_element_type=jnp.float32)
    partial_a = partial_a + jnp.einsum(
        "tc,dc->td", grad_key_raw, w_k, preferred_element_type=jnp.float32
    )
    partial_a = partial_a + jnp.einsum(
        "tc,dc->td", grad_value, w_v, preferred_element_type=jnp.float32
    )
    grad_a = tensor_grads(partial_a)
    part_gain_a = jnp.sum(grad_a * unit_a, axis=0)
    grad_x = grad_resid + norm_back(grad_a, gain_a.astype(jnp.float32), unit_a, inverse_a)
    grad_gain_a, grad_gain_f = gain_total(part_gain_a, part_gain_f)
    grads = (
        grad_gain_a,
        grad_w_q,
        grad_w_k,
        grad_w_v,
        grad_w_out,
        grad_gain_f,
        grad_e_gate,
        grad_e_up,
        grad_e_down,
        grad_d_gate,
        grad_d_up,
        grad_d_down,
    )
    return (grad_x, grads)


def body(
    tokens,
    place,
    lengths,
    expert_ids,
    gate_values,
    cotangent,
    gain_attn,
    w_query,
    w_key,
    w_value,
    w_out,
    gain_ffn,
    exp_gate,
    exp_up,
    exp_down,
    dense_gate,
    dense_up,
    dense_down,
):
    masters = (
        gain_attn,
        w_query,
        w_key,
        w_value,
        w_out,
        gain_ffn,
        exp_gate,
        exp_up,
        exp_down,
        dense_gate,
        dense_up,
        dense_down,
    )
    layer_count = gain_attn.shape[0]
    segment, position = layout(place[0], lengths[0])
    allowed = (segment[:, None] == segment[None, :]) & (position[None, :] <= position[:, None])
    cosine, sine = rope_tables(position, HD)
    state = tokens.astype(jnp.float32)
    kept_layers = []
    weight_layers = []
    for layer_index in range(layer_count):
        shards = tuple((master[layer_index].astype(jnp.bfloat16) for master in masters))
        weights = fetch_weights(shards)
        state, kept = forward_layer(
            state, weights, allowed, cosine, sine, expert_ids[layer_index], gate_values[layer_index]
        )
        kept_layers.append(kept)
        weight_layers.append(weights)
    mixed = state.astype(jnp.bfloat16)
    grad_state = cotangent.astype(jnp.float32)
    layer_grads = [None] * layer_count
    for layer_index in reversed(range(layer_count)):
        shards = tuple((master[layer_index].astype(jnp.bfloat16) for master in masters))
        weights = fetch_again(shards)
        grad_state, grads = backward_layer(
            grad_state, kept_layers[layer_index], weights, allowed, cosine, sine
        )
        layer_grads[layer_index] = sum_layer(grads)
    summed = tuple(
        (
            jnp.stack([layer_grads[level][member] for level in range(layer_count)])
            for member in range(12)
        )
    )
    return (
        mixed,
        grad_state,
        summed[0],
        summed[1],
        summed[2],
        summed[3],
        summed[4],
        summed[5],
        summed[6],
        summed[7],
        summed[8],
        summed[9],
        summed[10],
        summed[11],
    )


def solution(mesh):
    return jax.shard_map(
        body,
        mesh=mesh,
        in_specs=(
            P(("dp", "tensor"), None),
            P("dp", None),
            P("dp", None),
            P(None, "dp", None),
            P(None, "dp", None),
            P(("dp", "tensor"), None),
            P(None, "dp"),
            P(None, "dp", "tensor"),
            P(None, "dp", "tensor"),
            P(None, "dp", "tensor"),
            P(None, "tensor", "dp"),
            P(None, "dp"),
            P(None, None, "dp", "tensor"),
            P(None, None, "dp", "tensor"),
            P(None, None, "tensor", "dp"),
            P(None, "dp", "tensor"),
            P(None, "dp", "tensor"),
            P(None, "tensor", "dp"),
        ),
        out_specs=(
            P(("dp", "tensor"), None),
            P(("dp", "tensor"), None),
            P(None, "dp"),
            P(None, "dp", "tensor"),
            P(None, "dp", "tensor"),
            P(None, "dp", "tensor"),
            P(None, "tensor", "dp"),
            P(None, "dp"),
            P(None, None, "dp", "tensor"),
            P(None, None, "dp", "tensor"),
            P(None, None, "tensor", "dp"),
            P(None, "dp", "tensor"),
            P(None, "dp", "tensor"),
            P(None, "tensor", "dp"),
        ),
        check_vma=False,
    )
```

profile of v0, /device:TPU:9, one launch (start us, length us, event | category | flops | bytes accessed | tf_op | source)
XLA Modules:
  0.0 2570.8 jit_solution(5423822146261195364)
XLA Ops:
  12.3 15.9 all-reduce.15
  30.4 12.9 all_gather.121
  45.0 24.7 all-gather.1
  71.4 24.7 all-gather.2
  98.6 25.0 all-gather.3
  124.7 26.2 %all-gather.4 = bf16[1,192,768]{1,0,2:T(2,128)(2,1)S(1)} all-gather(bf16[1,192,96]{1,0,2:T(2,128)(2,1)S(1)} %get-tuple-element.150), channel_id=6, replica_groups=mesh['dp'=8,'tensor'=4] {'dp'}, dimensions={2}, use_global_device_ids=true | all-gather | bytes 331776 | tf_op jit(solution)/shard_map/all_gather | solution.py:100
  172.5 27.7 %all-gather.6 = bf16[1,768,512]{2,1,0:T(8,128)(2,1)} all-gather(bf16[1,96,512]{2,1,0:T(8,128)(2,1)S(1)} %get-tuple-element.138), channel_id=8, replica_groups=mesh['dp'=8,'tensor'=4] {'dp'}, dimensions={1}, use_global_device_ids=true | all-gather | bytes 884736 | tf_op jit(solution)/shard_map/all_gather | solution.py:105
  200.1 32.2 %all-gather.7 = bf16[1,768,512]{2,1,0:T(8,128)(2,1)} all-gather(bf16[1,96,512]{2,1,0:T(8,128)(2,1)S(1)} %get-tuple-element.140), channel_id=9, replica_groups=mesh['dp'=8,'tensor'=4] {'dp'}, dimensions={1}, use_global_device_ids=true | all-gather | bytes 884736 | tf_op jit(solution)/shard_map/all_gather | solution.py:106
  232.3 29.5 %all-gather.8 = bf16[1,512,768]{1,2,0:T(8,128)(2,1)} all-gather(bf16[1,512,96]{1,2,0:T(8,128)(2,1)S(1)} %get-tuple-element.136), channel_id=10, replica_groups=mesh['dp'=8,'tensor'=4] {'dp'}, dimensions={2}, use_global_device_ids=true | all-gather | bytes 884736 | tf_op jit(solution)/shard_map/all_gather | solution.py:107
  264.0 49.8 %all_gather.127 = bf16[512,768]{1,0:T(8,128)(2,1)S(1)} all-gather(bf16[128,768]{1,0:T(8,128)(2,1)S(1)} %multiply_convert_fusion.11), channel_id=1, replica_groups=mesh['dp'=8,'tensor'=4] {'tensor'}, dimensions={0}, use_global_device_ids=true | all-gather | bytes 983040 | tf_op jit(solution)/shard_map/all_gather | solution.py:71
  331.7 56.4 %all-gather.33.cloned.1.call-done = bf16[1,4,768,512]{3,2,1,0:T(8,128)(2,1)} async-done(((bf16[1,4,96,512]{3,2,1,0:T(8,128)(2,1)}), bf16[1,4,768,512]{3,2,1,0:T(8,128)(2,1)}) %all-gather.33.cloned.1.call-update) | async-done | bytes 3145744 | tf_op jit(solution)/shard_map/all_gather | solution.py:103
  400.0 28.3 %all-gather.16 = bf16[1,192,768]{1,0,2:T(2,128)(2,1)} all-gather(bf16[1,192,96]{1,0,2:T(2,128)(2,1)S(1)} %get-tuple-element.149), channel_id=18, replica_groups=mesh['dp'=8,'tensor'=4] {'dp'}, dimensions={2}, use_global_device_ids=true | all-gather | bytes 331776 | tf_op jit(solution)/shard_map/all_gather | solution.py:100
  431.1 29.6 %all-gather.14 = bf16[1,768,192]{2,1,0:T(8,128)(2,1)} all-gather(bf16[1,96,192]{2,1,0:T(8,128)(2,1)S(1)} %copy-done.98), channel_id=16, replica_groups=mesh['dp'=8,'tensor'=4] {'dp'}, dimensions={1}, use_global_device_ids=true | all-gather | bytes 331776 | tf_op jit(solution)/shard_map/all_gather | solution.py:97
  460.8 27.3 %all-gather.15 = bf16[1,768,192]{2,1,0:T(8,128)(2,1)} all-gather(bf16[1,96,192]{2,1,0:T(8,128)(2,1)S(1)} %copy-done.99), channel_id=17, replica_groups=mesh['dp'=8,'tensor'=4] {'dp'}, dimensions={1}, use_global_device_ids=true | all-gather | bytes 331776 | tf_op jit(solution)/shard_map/all_gather | solution.py:98
  488.0 27.6 %all-gather.13 = bf16[1,768,192]{2,1,0:T(8,128)(2,1)} all-gather(bf16[1,96,192]{2,1,0:T(8,128)(2,1)S(1)} %copy-done.97), channel_id=15, replica_groups=mesh['dp'=8,'tensor'=4] {'dp'}, dimensions={1}, use_global_device_ids=true | all-gather | bytes 331776 | tf_op jit(solution)/shard_map/all_gather | solution.py:99
  517.1 30.4 %all_gather.135 = bf16[512,768]{1,0:T(8,128)(2,1)S(1)} all-gather(bf16[128,768]{1,0:T(8,128)(2,1)S(1)} %multiply_convert_fusion.10), channel_id=1, replica_groups=mesh['dp'=8,'tensor'=4] {'tensor'}, dimensions={0}, use_global_device_ids=true | all-gather | bytes 983040 | tf_op jit(solution)/shard_map/all_gather | solution.py:71
  558.7 10.2 all_gather.148
  569.0 30.6 %all-gather.18 = bf16[1,768,512]{2,1,0:T(8,128)(2,1)} all-gather(bf16[1,96,512]{2,1,0:T(8,128)(2,1)} %get-tuple-element.137), channel_id=20, replica_groups=mesh['dp'=8,'tensor'=4] {'dp'}, dimensions={1}, use_global_device_ids=true | all-gather | bytes 884736 | tf_op jit(solution)/shard_map/all_gather | solution.py:105
  599.6 30.1 %all-gather.19 = bf16[1,768,512]{2,1,0:T(8,128)(2,1)} all-gather(bf16[1,96,512]{2,1,0:T(8,128)(2,1)} %get-tuple-element.139), channel_id=21, replica_groups=mesh['dp'=8,'tensor'=4] {'dp'}, dimensions={1}, use_global_device_ids=true | all-gather | bytes 884736 | tf_op jit(solution)/shard_map/all_gather | solution.py:106
  629.7 30.3 %all-gather.20 = bf16[1,512,768]{1,2,0:T(8,128)(2,1)} all-gather(bf16[1,512,96]{1,2,0:T(8,128)(2,1)} %get-tuple-element.135), channel_id=22, replica_groups=mesh['dp'=8,'tensor'=4] {'dp'}, dimensions={2}, use_global_device_ids=true | all-gather | bytes 884736 | tf_op jit(solution)/shard_map/all_gather | solution.py:107
  674.6 25.3 all_gather.141
  712.9 8.0 fusion.1
  728.5 23.2 reduce-scatter.37.cloned.1.call-done
  755.7 8.9 all_gather.149
  778.2 17.2 reduce-scatter.39.cloned.1.call-done
  797.7 23.6 reduce-scatter.35.cloned.1.call-done
  823.8 8.7 all_gather.150
  850.8 20.1 reduce-scatter.41.cloned.1.call-done
  873.4 8.7 all_gather.151
  946.6 7.9 copy.132
  974.4 7.9 copy.130
  1000.8 202.6 %reduce-scatter.47.cloned.1.call-done = f32[96,192]{1,0:T(8,128)} async-done(((f32[768,192]{1,0:T(8,128)}), f32[96,192]{1,0:T(8,128)}) %reduce-scatter.47.cloned.1.call-update) | async-done | bytes 73744 | tf_op jit(solution)/shard_map/reduce_scatter | solution.py:131
  1203.4 167.2 %reduce-scatter.45.cloned.1.call-done = f32[96,192]{1,0:T(8,128)} async-done(((f32[768,192]{1,0:T(8,128)}), f32[96,192]{1,0:T(8,128)}) %reduce-scatter.45.cloned.1.call-update) | async-done | bytes 73744 | tf_op jit(solution)/shard_map/reduce_scatter | solution.py:131
  1372.3 100.5 %reduce-scatter.51.cloned.1.call-done = f32[96,192]{1,0:T(8,128)} async-done(((f32[768,192]{1,0:T(8,128)}), f32[96,192]{1,0:T(8,128)}) %reduce-scatter.51.cloned.1.call-update) | async-done | bytes 73744 | tf_op jit(solution)/shard_map/reduce_scatter | solution.py:132
  1472.8 206.1 %reduce-scatter.49.cloned.1.call-done = f32[96,192]{1,0:T(8,128)} async-done(((f32[768,192]{1,0:T(8,128)}), f32[96,192]{1,0:T(8,128)}) %reduce-scatter.49.cloned.1.call-update) | async-done | bytes 73744 | tf_op jit(solution)/shard_map/reduce_scatter | solution.py:132
  1680.5 131.6 %reduce-scatter.55.cloned.1.call-done = f32[96,192]{1,0:T(8,128)} async-done(((f32[768,192]{1,0:T(8,128)}), f32[96,192]{1,0:T(8,128)}) %reduce-scatter.55.cloned.1.call-update) | async-done | bytes 73744 | tf_op jit(solution)/shard_map/reduce_scatter | solution.py:133
  1812.1 64.6 %reduce-scatter.53.cloned.1.call-done = f32[96,192]{1,0:T(8,128)} async-done(((f32[768,192]{1,0:T(8,128)}), f32[96,192]{1,0:T(8,128)}) %reduce-scatter.53.cloned.1.call-update) | async-done | bytes 73744 | tf_op jit(solution)/shard_map/reduce_scatter | solution.py:133
  1879.0 24.5 reduce-scatter.43.cloned.1.call-done
  1904.8 27.6 %all-reduce.12 = (f32[768]{0:T(1024)S(1)}, f32[768]{0:T(1024)S(1)}, f32[768]{0:T(1024)S(1)}, f32[768]{0:T(1024)S(1)}) all-reduce(f32[768]{0:T(1024)S(1)} %copy-done.110, f32[768]{0:T(1024)S(1)} %get-tuple-element.76, f32[768]{0:T(1024)S(1)} %copy-done.109, ...), channel_id=35, replica_groups=mesh['dp'=8,'tensor'=4] {'dp'}, use_global_device_ids=true, to_apply=%region_32.33.clone | all-reduce | flops 3072 | bytes 24576
  1932.7 12.8 all-reduce.14
  1946.7 24.3 reduce-scatter.63.cloned.1.call-done
  1971.0 68.0 %reduce-scatter.61.cloned.1.call-done = f32[96,512]{1,0:T(8,128)} async-done(((f32[768,512]{1,0:T(8,128)}), f32[96,512]{1,0:T(8,128)}) %reduce-scatter.61.cloned.1.call-update) | async-done | bytes 196624 | tf_op jit(solution)/shard_map/reduce_scatter | solution.py:139
  2040.8 66.1 %reduce-scatter.67.cloned.1.call-done = f32[96,512]{1,0:T(8,128)} async-done(((f32[768,512]{1,0:T(8,128)}), f32[96,512]{1,0:T(8,128)}) %reduce-scatter.67.cloned.1.call-update) | async-done | bytes 196624 | tf_op jit(solution)/shard_map/reduce_scatter | solution.py:140
  2106.9 67.1 %reduce-scatter.65.cloned.1.call-done = f32[96,512]{1,0:T(8,128)} async-done(((f32[768,512]{1,0:T(8,128)}), f32[96,512]{1,0:T(8,128)}) %reduce-scatter.65.cloned.1.call-update) | async-done | bytes 196624 | tf_op jit(solution)/shard_map/reduce_scatter | solution.py:140
  2175.8 65.8 %reduce-scatter.71.cloned.1.call-done = f32[512,96]{0,1:T(8,128)} async-done(((f32[512,768]{0,1:T(8,128)}), f32[512,96]{0,1:T(8,128)}) %reduce-scatter.71.cloned.1.call-update) | async-done | bytes 196624 | tf_op jit(solution)/shard_map/reduce_scatter | solution.py:141
  2241.6 67.2 %reduce-scatter.69.cloned.1.call-done = f32[512,96]{0,1:T(8,128)} async-done(((f32[512,768]{0,1:T(8,128)}), f32[512,96]{0,1:T(8,128)}) %reduce-scatter.69.cloned.1.call-update) | async-done | bytes 196624 | tf_op jit(solution)/shard_map/reduce_scatter | solution.py:141
  2312.6 118.2 %reduce-scatter.59.cloned.1.call-done = f32[4,512,96]{1,2,0:T(8,128)} async-done(((f32[4,512,768]{1,2,0:T(8,128)}), f32[4,512,96]{1,2,0:T(8,128)}) %reduce-scatter.59.cloned.1.call-update) | async-done | bytes 786448 | tf_op jit(solution)/shard_map/reduce_scatter | solution.py:138
  2430.8 121.0 %reduce-scatter.57.cloned.1.call-done = f32[4,512,96]{1,2,0:T(8,128)} async-done(((f32[4,512,768]{1,2,0:T(8,128)}), f32[4,512,96]{1,2,0:T(8,128)}) %reduce-scatter.57.cloned.1.call-update) | async-done | bytes 786448 | tf_op jit(solution)/shard_map/reduce_scatter | solution.py:138
  (533 shorter events, 287.3 us)
Async XLA Ops:
  8.0 253.8 %reduce-scatter.29.cloned.1.call-start = ((), (), s32[]{:S(2)}) async-start(), calls=%async_computation.24 | async-start | bytes 983040 | tf_op jit(solution)/shard_map/reduce_scatter | solution.py:79
  29.2 68.5 %copy-start.126 = (s32[1,3]{1,0:T(1,128)S(1)}, s32[1,3]{1,0:T(1,128)}, u32[]{:S(2)}) copy-start(s32[1,3]{1,0:T(1,128)} %param.20) | copy-start | bytes 40
  29.2 68.6 %copy-start.108 = (s32[1,512]{1,0:T(1,128)S(1)}, s32[1,512]{1,0:T(1,128)}, u32[]{:S(2)}) copy-start(s32[1,512]{1,0:T(1,128)} %param.19) | copy-start | bytes 6148
  29.2 68.7 %copy-start.95 = (f32[2,96,192]{2,1,0:T(8,128)S(1)}, f32[2,96,192]{2,1,0:T(8,128)}, u32[]{:S(2)}) copy-start(f32[2,96,192]{2,1,0:T(8,128)} %param.26) | copy-start | bytes 442372
  43.3 80.8 %copy-start.2 = (bf16[512,768]{1,0:T(8,128)(2,1)}, bf16[512,768]{1,0:T(8,128)(2,1)S(1)}, u32[]{:S(2)}) copy-start(bf16[512,768]{1,0:T(8,128)(2,1)S(1)} %all_gather.121) | copy-start | bytes 2359300
  156.7 161.9 %all-gather.35.cloned.1.call-start = ((), (), s32[]{:S(2)}) async-start(), calls=%async_computation.48 | async-start | bytes 3538944 | tf_op jit(solution)/shard_map/all_gather | solution.py:104
  160.4 165.4 %all-gather.31.cloned.1.call-start = ((), (), s32[]{:S(2)}) async-start(), calls=%async_computation.46 | async-start | bytes 3538944 | tf_op jit(solution)/shard_map/all_gather | solution.py:102
  163.0 225.2 %all-gather.33.cloned.1.call-start = ((), (), s32[]{:S(2)}) async-start(), calls=%async_computation.47 | async-start | bytes 3538944 | tf_op jit(solution)/shard_map/all_gather | solution.py:103
  165.5 96.3 %copy-start.8 = (bf16[128,768]{1,0:T(8,128)(2,1)S(1)}, bf16[128,768]{1,0:T(8,128)(2,1)}, u32[]{:S(2)}) copy-start(bf16[128,768]{1,0:T(8,128)(2,1)} %param.18) | copy-start | bytes 589828
  165.5 350.1 %reduce-scatter.31.cloned.1.call-start = ((), (), s32[]{:S(2)}) async-start(), calls=%async_computation.25 | async-start | bytes 983040 | tf_op jit(solution)/shard_map/reduce_scatter | solution.py:79
  324.6 63.5 %copy-start.113 = (f32[512,4]{0,1:T(4,128)S(1)}, f32[512,4]{0,1:T(4,128)}, u32[]{:S(2)}) copy-start(f32[512,4]{0,1:T(4,128)} %select_reduce_fusion.1) | copy-start | bytes 24580
  397.6 63.1 %copy-start.99 = (bf16[1,96,192]{2,1,0:T(8,128)(2,1)S(1)}, bf16[1,96,192]{2,1,0:T(8,128)(2,1)}, u32[]{:S(2)}) copy-start(bf16[1,96,192]{2,1,0:T(8,128)(2,1)} %get-tuple-element.153) | copy-start | bytes 110596
  397.6 90.4 %copy-start.97 = (bf16[1,96,192]{2,1,0:T(8,128)(2,1)S(1)}, bf16[1,96,192]{2,1,0:T(8,128)(2,1)}, u32[]{:S(2)}) copy-start(bf16[1,96,192]{2,1,0:T(8,128)(2,1)} %get-tuple-element.155) | copy-start | bytes 110596
  399.2 260.8 %all-gather.41.cloned.1.call-start = ((), (), s32[]{:S(2)}) async-start(), calls=%async_computation.51 | async-start | bytes 3538944 | tf_op jit(solution)/shard_map/all_gather | solution.py:104
  399.9 272.0 %reduce-scatter.33.cloned.1.call-start = ((), (), s32[]{:S(2)}) async-start(), calls=%async_computation.26 | async-start | bytes 983040 | tf_op jit(solution)/shard_map/reduce_scatter | solution.py:79
  400.0 149.3 %copy-start.102 = (f32[768]{0:T(1024)}, f32[768]{0:T(1024)S(1)}, u32[]{:S(2)}) copy-start(f32[768]{0:T(1024)S(1)} %convert_element_type.437) | copy-start | bytes 9220
  555.8 151.2 %all-gather.37.cloned.1.call-start = ((), (), s32[]{:S(2)}) async-start(), calls=%async_computation.49 | async-start | bytes 3538944 | tf_op jit(solution)/shard_map/all_gather | solution.py:102
  556.6 156.3 %all-gather.39.cloned.1.call-start = ((), (), s32[]{:S(2)}) async-start(), calls=%async_computation.50 | async-start | bytes 3538944 | tf_op jit(solution)/shard_map/all_gather | solution.py:103
  557.3 194.4 %reduce-scatter.37.cloned.1.call-start = ((), (), s32[]{:S(2)}) async-start(), calls=%async_computation.28 | async-start | bytes 983040 | tf_op jit(solution)/shard_map/reduce_scatter | solution.py:85
  727.7 67.7 %reduce-scatter.39.cloned.1.call-start = ((), (), s32[]{:S(2)}) async-start(), calls=%async_computation.29 | async-start | bytes 983040 | tf_op jit(solution)/shard_map/reduce_scatter | solution.py:85
  772.1 49.2 %reduce-scatter.35.cloned.1.call-start = ((), (), s32[]{:S(2)}) async-start(), calls=%async_computation.27 | async-start | bytes 983040 | tf_op jit(solution)/shard_map/reduce_scatter | solution.py:79
  778.2 92.7 %reduce-scatter.41.cloned.1.call-start = ((), (), s32[]{:S(2)}) async-start(), calls=%async_computation.30 | async-start | bytes 983040 | tf_op jit(solution)/shard_map/reduce_scatter | solution.py:85
  847.6 149.2 %reduce-scatter.75.cloned.1.call-start = ((), (), s32[]{:S(2)}) async-start(), calls=%async_computation.53 | async-start | bytes 884736
  850.7 149.1 %reduce-scatter.73.cloned.1.call-start = ((), (), s32[]{:S(2)}) async-start(), calls=%async_computation.52 | async-start | bytes 884736
  885.3 318.2 %reduce-scatter.47.cloned.1.call-start = ((), (), s32[]{:S(2)}) async-start(), calls=%async_computation.33 | async-start | bytes 884736 | tf_op jit(solution)/shard_map/reduce_scatter | solution.py:131
  888.5 482.1 %reduce-scatter.45.cloned.1.call-start = ((), (), s32[]{:S(2)}) async-start(), calls=%async_computation.32 | async-start | bytes 884736 | tf_op jit(solution)/shard_map/reduce_scatter | solution.py:131
  896.7 576.0 %reduce-scatter.51.cloned.1.call-start = ((), (), s32[]{:S(2)}) async-start(), calls=%async_computation.35 | async-start | bytes 884736 | tf_op jit(solution)/shard_map/reduce_scatter | solution.py:132
  899.3 779.6 %reduce-scatter.49.cloned.1.call-start = ((), (), s32[]{:S(2)}) async-start(), calls=%async_computation.34 | async-start | bytes 884736 | tf_op jit(solution)/shard_map/reduce_scatter | solution.py:132
  903.4 908.7 %reduce-scatter.55.cloned.1.call-start = ((), (), s32[]{:S(2)}) async-start(), calls=%async_computation.37 | async-start | bytes 884736 | tf_op jit(solution)/shard_map/reduce_scatter | solution.py:133
  906.0 970.7 %reduce-scatter.53.cloned.1.call-start = ((), (), s32[]{:S(2)}) async-start(), calls=%async_computation.36 | async-start | bytes 884736 | tf_op jit(solution)/shard_map/reduce_scatter | solution.py:133
  909.7 993.8 %reduce-scatter.43.cloned.1.call-start = ((), (), s32[]{:S(2)}) async-start(), calls=%async_computation.31 | async-start | bytes 983040 | tf_op jit(solution)/shard_map/reduce_scatter | solution.py:85
  913.3 1057.7 %reduce-scatter.63.cloned.1.call-start = ((), (), s32[]{:S(2)}) async-start(), calls=%async_computation.41 | async-start | bytes 1769472 | tf_op jit(solution)/shard_map/reduce_scatter | solution.py:139
  916.2 1122.8 %reduce-scatter.61.cloned.1.call-start = ((), (), s32[]{:S(2)}) async-start(), calls=%async_computation.40 | async-start | bytes 1769472 | tf_op jit(solution)/shard_map/reduce_scatter | solution.py:139
  918.1 1188.8 %reduce-scatter.67.cloned.1.call-start = ((), (), s32[]{:S(2)}) async-start(), calls=%async_computation.43 | async-start | bytes 1769472 | tf_op jit(solution)/shard_map/reduce_scatter | solution.py:140
  919.9 1254.1 %reduce-scatter.65.cloned.1.call-start = ((), (), s32[]{:S(2)}) async-start(), calls=%async_computation.42 | async-start | bytes 1769472 | tf_op jit(solution)/shard_map/reduce_scatter | solution.py:140
  921.7 1319.9 %reduce-scatter.71.cloned.1.call-start = ((), (), s32[]{:S(2)}) async-start(), calls=%async_computation.45 | async-start | bytes 1769472 | tf_op jit(solution)/shard_map/reduce_scatter | solution.py:141
  924.7 1384.1 %reduce-scatter.69.cloned.1.call-start = ((), (), s32[]{:S(2)}) async-start(), calls=%async_computation.44 | async-start | bytes 1769472 | tf_op jit(solution)/shard_map/reduce_scatter | solution.py:141
  927.6 1503.2 %reduce-scatter.59.cloned.1.call-start = ((), (), s32[]{:S(2)}) async-start(), calls=%async_computation.39 | async-start | bytes 7077888 | tf_op jit(solution)/shard_map/reduce_scatter | solution.py:138
  934.1 1617.7 %reduce-scatter.57.cloned.1.call-start = ((), (), s32[]{:S(2)}) async-start(), calls=%async_computation.38 | async-start | bytes 7077888 | tf_op jit(solution)/shard_map/reduce_scatter | solution.py:138
  940.5 1614.0 %all-reduce.18.cloned.1.call-start = ((), (), s32[]{:S(2)}) async-start(), calls=%async_computation.54 | async-start | bytes 50331648
  996.0 907.5 %copy-start.101 = (f32[768]{0:T(1024)S(1)}, f32[768]{0:T(1024)}, u32[]{:S(2)}) copy-start(f32[768]{0:T(1024)} %copy-done.100) | copy-start | bytes 9220
  996.0 907.5 %copy-start.121 = (f32[128]{0:T(128)S(1)}, f32[128]{0:T(128)}, u32[]{:S(2)}) copy-start(f32[128]{0:T(128)} %copy-done.120) | copy-start | bytes 1540
  996.1 908.7 %copy-start.109 = (f32[768]{0:T(1024)S(1)}, f32[768]{0:T(1024)}, u32[]{:S(2)}) copy-start(f32[768]{0:T(1024)} %get-tuple-element.70) | copy-start | bytes 9220
  996.1 908.7 %copy-start.110 = (f32[768]{0:T(1024)S(1)}, f32[768]{0:T(1024)}, u32[]{:S(2)}) copy-start(f32[768]{0:T(1024)} %get-tuple-element.74) | copy-start | bytes 9220
  996.1 1314.5 %copy-start.22 = (f32[128,768]{1,0:T(8,128)S(1)}, f32[128,768]{1,0:T(8,128)}, u32[]{:S(2)}) copy-start(f32[128,768]{1,0:T(8,128)} %get-tuple-element.97) | copy-start | bytes 1179652
  996.1 1314.5 %copy-start.63 = (bf16[128,768]{1,0:T(8,128)(2,1)S(1)}, bf16[128,768]{1,0:T(8,128)(2,1)}, u32[]{:S(2)}) copy-start(bf16[128,768]{1,0:T(8,128)(2,1)} %reduce-scatter.41.cloned.1.call-done) | copy-start | bytes 589828
  996.1 1314.5 %copy-start.117 = (f32[128]{0:T(128)S(1)}, f32[128]{0:T(128)}, u32[]{:S(2)}) copy-start(f32[128]{0:T(128)} %copy-done.115) | copy-start | bytes 1540
  996.1 1314.5 %copy-start.124 = (f32[128]{0:T(128)S(1)}, f32[128]{0:T(128)}, u32[]{:S(2)}) copy-start(f32[128]{0:T(128)} %copy-done.123) | copy-start | bytes 1540
  (120 other events, 908.0 us)
Sparse Core Ops, SparseCore 0:
  156.8 46.0 reduce-scatter.28
  399.3 23.3 reduce-scatter.30
  556.0 24.3 reduce-scatter.32
  727.9 23.8 reduce-scatter.36
  772.3 23.1 reduce-scatter.38
  798.0 23.2 reduce-scatter.34
  847.8 23.0 reduce-scatter.40
  874.6 60.4 reduce-scatter.74
  938.4 61.4 reduce-scatter.72
  1003.4 200.0 reduce-scatter.46
  1206.7 163.8 reduce-scatter.44
  1374.2 98.5 reduce-scatter.50
  1476.1 202.7 reduce-scatter.48
  1682.4 129.6 reduce-scatter.54
  1815.2 61.4 reduce-scatter.52
  1879.3 24.2 reduce-scatter.42
  1907.8 63.1 reduce-scatter.62
  1974.8 64.1 reduce-scatter.60
  2043.4 63.4 reduce-scatter.66
  2110.1 63.7 reduce-scatter.64
  2177.8 63.7 reduce-scatter.70
  2245.0 63.7 reduce-scatter.68
  2312.9 117.9 reduce-scatter.58
  2434.7 117.0 reduce-scatter.56
Sparse Core Ops, SparseCore 1:
  160.5 99.4 all-gather.34
  262.8 62.9 all-gather.30
  328.6 59.4 all-gather.32
  402.4 70.2 all-gather.40
  559.6 79.5 all-gather.36
  642.2 62.0 all-gather.38
  996.2 777.9 all-reduce.17
where the time goes:
time: 2580 us; the launch traced here: 2570 us
  waiting for transfers between devices  1640 us (64%)
  blocking collectives  605 us (23%)
  matrix products  163 us (6%)
  local copies, waits for them, and re-layouts  83.6 us (3%)
  other arithmetic  56.8 us (2%)
    reduce_scatter x2, waiting for transfers between devices, sum_layer(): lax.psum_scatter(grads[1], 'dp', scatter_dimension=0, tiled=True)  370 us
    reduce_scatter x2, waiting for transfers between devices, sum_layer(): lax.psum_scatter(grads[2], 'dp', scatter_dimension=0, tiled=True)  307 us
    reduce_scatter x2, waiting for transfers between devices, sum_layer(): lax.psum_scatter(grads[8], 'dp', scatter_dimension=2, tiled=True)  239 us
    reduce_scatter x2, waiting for transfers between devices, sum_layer(): lax.psum_scatter(grads[3], 'dp', scatter_dimension=0, tiled=True)  196 us
    reduce_scatter x2, waiting for transfers between devices, sum_layer(): lax.psum_scatter(grads[10], 'dp', scatter_dimension=0, tiled=True)  133 us
    reduce_scatter x2, waiting for transfers between devices, sum_layer(): lax.psum_scatter(grads[11], 'dp', scatter_dimension=1, tiled=True)  133 us
    all_gather x4, blocking collectives, gather_normed(): return lax.all_gather(rows, 'tensor', axis=0, tiled=True)  118 us
    reduce_scatter x2, waiting for transfers between devices, sum_layer(): lax.psum_scatter(grads[9], 'dp', scatter_dimension=0, tiled=True)  92.3 us
  transfers between devices with their start and end apart: 31, of which 22 were waited for; matrix products, arithmetic and copies ran while one was open for 8% of the time, Pallas kernels for 0%

commit v1 on v0

v1 whole, which is shorter than its diff:
```python
import functools

import jax
import jax.numpy as jnp
from jax import lax
from jax.experimental import pallas as pl
from jax.experimental.pallas import tpu as pltpu
from jax.sharding import PartitionSpec as P

HD = 64
EPSILON = 1e-06
MASKED_SCORE = -1e30
MESH = pl.DeviceIdType.MESH
ANY = pl.BlockSpec(memory_space=pl.ANY)
VMEM = pl.BlockSpec(memory_space=pltpu.VMEM)
F32 = jnp.float32
BF16 = jnp.bfloat16


def split_dp(dp):
    inner = 2 ** ((dp.bit_length() - 1) // 2)
    return dp // inner, inner


def place_of(inner):
    d = lax.axis_index("dp")
    return lax.div(d, inner), lax.rem(d, inner), lax.axis_index("tensor")


def across(t):
    return lax.rem(t + 2, 4), t + 1 - 2 * lax.rem(t, 2)


def meet(devices):
    barrier = pltpu.get_barrier_semaphore()
    for device in devices:
        pl.semaphore_signal(barrier, inc=1, device_id=device, device_id_type=MESH)
    pl.semaphore_wait(barrier, len(devices))


def send(source, target, send_sem, recv_sem, device):
    copy = pltpu.make_async_remote_copy(
        src_ref=source,
        dst_ref=target,
        send_sem=send_sem,
        recv_sem=recv_sem,
        device_id=device,
        device_id_type=MESH,
    )
    copy.start()
    return copy


def gather_kernel(outer, inner, own, out, zs, zr, ys, yr, cs, cr, ls):
    dz, dx, t = place_of(inner)
    d = lax.axis_index("dp")
    ty, tc = across(t)
    zdev = [(lax.rem(dz + k, outer) * inner + dx, t) for k in range(1, outer)]
    meet(zdev + [(d, ty), (d, tc)])
    mine = pltpu.make_async_copy(own, out.at[dz, t], ls)
    mine.start()
    zc = [
        send(own, out.at[dz, t], zs.at[k], zr.at[k], dev) for k, dev in enumerate(zdev)
    ]
    yc = [send(own, out.at[dz, t], ys.at[0], yr.at[0], (d, ty))]
    cc = [send(own, out.at[dz, t], cs.at[0], cr.at[0], (d, tc))]

    def second(k, source):
        yc[k].wait_recv()
        block = out.at[source, ty]
        at = outer + k
        cc.append(send(block, block, cs.at[at], cr.at[at], (d, tc)))

    before = dz
    for k in range(1, outer):
        source = lax.rem(dz - k + outer, outer)
        zc[k - 1].wait_recv()
        block = out.at[source, t]
        yc.append(send(block, block, ys.at[k], yr.at[k], (d, ty)))
        cc.append(send(block, block, cs.at[k], cr.at[k], (d, tc)))
        second(k - 1, before)
        before = source
    second(outer - 1, before)
    for copy in cc:
        copy.wait_recv()
    for copy in zc + yc + cc:
        copy.wait_send()
    mine.wait()


def gather(own, outer, inner, ident):
    dma = pltpu.SemaphoreType.DMA
    return pl.pallas_call(
        functools.partial(gather_kernel, outer, inner),
        out_shape=jax.ShapeDtypeStruct((outer, 4) + own.shape, own.dtype),
        in_specs=[VMEM],
        out_specs=ANY,
        scratch_shapes=[
            dma((max(outer - 1, 1),)),
            dma((max(outer - 1, 1),)),
            dma((outer,)),
            dma((outer,)),
            dma((2 * outer,)),
            dma((2 * outer,)),
            dma,
        ],
        compiler_params=pltpu.CompilerParams(collective_id=ident, has_side_effects=True),
        name="gather",
    )(own)


def scatter_kernel(
    outer, inner, part, out, from_c, sum_c, from_y, sum_y, from_z, cs, cr, ys, yr, zs, zr
):
    dz, dx, t = place_of(inner)
    d = lax.axis_index("dp")
    ty, tc = across(t)
    y, c = lax.div(t, 2), lax.rem(t, 2)
    zdev = [(lax.rem(dz + k, outer) * inner + dx, t) for k in range(1, outer)]
    meet(zdev + [(d, ty), (d, tc)])
    order = list(range(1, outer)) + [0]
    where = [lax.rem(dz + k, outer) for k in range(outer)]
    cc, yc, zc = {}, {}, {}
    for k in order:
        cc[k] = send(
            part.at[where[k], :, 1 - c], from_c.at[k], cs.at[k], cr.at[k], (d, tc)
        )

    def finish(k):
        yc[k].wait_recv()
        total = sum_c[k, y].astype(F32) + from_y[k].astype(F32)
        if k == 0:
            return total
        sum_y[k] = total.astype(BF16)
        zc[k] = send(
            sum_y.at[k], from_z.at[k - 1], zs.at[k - 1], zr.at[k - 1], zdev[k - 1]
        )
        return None

    last = None
    for k in order:
        cc[k].wait_recv()
        sum_c[k] = (part[where[k], :, c].astype(F32) + from_c[k].astype(F32)).astype(BF16)
        yc[k] = send(sum_c.at[k, 1 - y], from_y.at[k], ys.at[k], yr.at[k], (d, ty))
        if last is not None:
            finish(last)
        last = k
    total = finish(last)
    for k in order[:-1]:
        zc[k].wait_recv()
        total = total + from_z[k - 1].astype(F32)
    out[...] = total
    for group in (cc, yc, zc):
        for k in group:
            group[k].wait_send()


def scatter(part, outer, inner, ident):
    dma = pltpu.SemaphoreType.DMA
    rows, width = part.shape[-2:]
    low = max(outer - 1, 1)
    return pl.pallas_call(
        functools.partial(scatter_kernel, outer, inner),
        out_shape=jax.ShapeDtypeStruct((rows, width), F32),
        in_specs=[VMEM],
        out_specs=VMEM,
        scratch_shapes=[
            pltpu.VMEM((outer, 2, rows, width), BF16),
            pltpu.VMEM((outer, 2, rows, width), BF16),
            pltpu.VMEM((outer, rows, width), BF16),
            pltpu.VMEM((outer, rows, width), BF16),
            pltpu.VMEM((low, rows, width), BF16),
            dma((outer,)),
            dma((outer,)),
            dma((outer,)),
            dma((outer,)),
            dma((low,)),
            dma((low,)),
        ],
        compiler_params=pltpu.CompilerParams(collective_id=ident, has_side_effects=True),
        name="scatter",
    )(part)


def fetch_kernel(outer, inner, count, *refs):
    owns, outs, holds = refs[:count], refs[count : 2 * count], refs[2 * count : 3 * count]
    zs, zr, xs, xr, ls = refs[3 * count :]
    dz, dx, t = place_of(inner)
    d = lax.axis_index("dp")
    zdev = [(lax.rem(dz + k, outer) * inner + dx, t) for k in range(1, outer)]
    xdev = [(dz * inner + lax.rem(dx + j, inner), t) for j in range(1, inner)]
    meet(zdev + xdev)
    zc, xc, into, back = {}, [], [], []
    for i in range(count):
        spread = owns[i].shape[0] == outer
        here = owns[i].at[dz if spread else 0]
        into.append(pltpu.make_async_copy(here, holds[i], ls.at[i]))
        into[i].start()
        for k in range(1, outer):
            there = owns[i].at[lax.rem(dz + k, outer) if spread else 0]
            at = i * outer + k
            zc[i, k] = send(there, outs[i].at[d], zs.at[at], zr.at[at], zdev[k - 1])
        for j in range(1, inner):
            at = i * outer * inner + j
            xc.append(send(here, outs[i].at[d], xs.at[at], xr.at[at], xdev[j - 1]))
    for i in range(count):
        into[i].wait()
        back.append(pltpu.make_async_copy(holds[i], outs[i].at[d], ls.at[i]))
        back[i].start()
        for k in range(1, outer):
            zc[i, k].wait_recv()
            block = outs[i].at[lax.rem(dz - k + outer, outer) * inner + dx]
            for j in range(1, inner):
                at = (i * outer + k) * inner + j
                xc.append(send(block, block, xs.at[at], xr.at[at], xdev[j - 1]))
    for copy in xc:
        copy.wait_recv()
        copy.wait_send()
    for key in zc:
        zc[key].wait_send()
    for copy in back:
        copy.wait()


def fetch(owns, outer, inner, ident):
    dma = pltpu.SemaphoreType.DMA
    count = len(owns)
    dp = outer * inner
    return pl.pallas_call(
        functools.partial(fetch_kernel, outer, inner, count),
        out_shape=[jax.ShapeDtypeStruct((dp,) + own.shape[1:], own.dtype) for own in owns],
        in_specs=[ANY] * count,
        out_specs=[ANY] * count,
        scratch_shapes=[pltpu.VMEM(own.shape[1:], own.dtype) for own in owns]
        + [
            dma((count * outer,)),
            dma((count * outer,)),
            dma((count * dp,)),
            dma((count * dp,)),
            dma((count,)),
        ],
        compiler_params=pltpu.CompilerParams(collective_id=ident, has_side_effects=True),
        name="fetch",
    )(*owns)


def push_kernel(outer, inner, count, *refs):
    parts, outs = refs[:count], refs[count : 2 * count]
    froms, sums = refs[2 * count : 3 * count], refs[3 * count : 4 * count]
    xs, xr, zs, zr = refs[4 * count :]
    dz, dx, t = place_of(inner)
    zdev = [(lax.rem(dz + k, outer) * inner + dx, t) for k in range(1, outer)]
    xdev = [(dz * inner + lax.rem(dx + j, inner), t) for j in range(1, inner)]
    meet(zdev + xdev)
    order = list(range(1, outer)) + [0]
    xc, zc = {}, {}
    for i in range(count):
        for k in order:
            for j in range(1, inner):
                slot = lax.rem(dz + k, outer) * inner + lax.rem(dx + j, inner)
                at = (i * outer + k) * inner + j
                xc[i, k, j] = send(
                    parts[i].at[slot],
                    froms[i].at[j - 1, k],
                    xs.at[at],
                    xr.at[at],
                    xdev[j - 1],
                )
    for i in range(count):
        for k in order:
            slot = lax.rem(dz + k, outer) * inner + dx
            total = parts[i][slot].astype(F32)
            for j in range(1, inner):
                xc[i, k, j].wait_recv()
                total = total + froms[i][j - 1, k].astype(F32)
            total = total.astype(parts[i].dtype)
            if k:
                sums[i][k - 1] = total
                at = i * outer + k
                zc[i, k] = send(
                    sums[i].at[k - 1], outs[i].at[dz], zs.at[at], zr.at[at], zdev[k - 1]
                )
            else:
                outs[i][dz] = total
    for key in zc:
        zc[key].wait_recv()
        zc[key].wait_send()
    for key in xc:
        xc[key].wait_send()


def push(parts, outer, inner, ident):
    dma = pltpu.SemaphoreType.DMA
    count = len(parts)
    dp = outer * inner
    return pl.pallas_call(
        functools.partial(push_kernel, outer, inner, count),
        out_shape=[jax.ShapeDtypeStruct((outer,) + p.shape[1:], p.dtype) for p in parts],
        in_specs=[VMEM] * count,
        out_specs=[VMEM] * count,
        scratch_shapes=[pltpu.VMEM((inner - 1, outer) + p.shape[1:], p.dtype) for p in parts]
        + [pltpu.VMEM((outer - 1,) + p.shape[1:], p.dtype) for p in parts]
        + [
            dma((count * dp,)),
            dma((count * dp,)),
            dma((count * outer,)),
            dma((count * outer,)),
        ],
        compiler_params=pltpu.CompilerParams(collective_id=ident, has_side_effects=True),
        name="push",
    )(*parts)


def layout(place_row, length_row):
    ends = jnp.cumsum(length_row, dtype=jnp.int32)
    after = place_row[:, None] >= ends[None, :]
    segment = jnp.sum(after.astype(jnp.int32), axis=1, dtype=jnp.int32)
    begins = jnp.sum(jnp.where(after, length_row[None, :], 0), axis=1, dtype=jnp.int32)
    return (segment, place_row - begins)


def rope_tables(position, width):
    half_width = width // 2
    freqs = 10000.0 ** (-jnp.arange(half_width, dtype=F32) / half_width)
    angles = position.astype(F32)[:, None] * freqs[None, :]
    return (jnp.cos(angles)[:, None, :], jnp.sin(angles)[:, None, :])


def rotate(values, cosine, sine):
    half_width = values.shape[-1] // 2
    first_half = values[..., :half_width]
    second_half = values[..., half_width:]
    return jnp.concatenate(
        [first_half * cosine - second_half * sine, first_half * sine + second_half * cosine],
        axis=-1,
    )


def normed(values):
    inverse = lax.rsqrt(jnp.mean(values * values, axis=-1, keepdims=True) + EPSILON)
    return (values * inverse, inverse)


def norm_back(grad_normed, gain_row, unit_rows, inverse):
    scaled = grad_normed * gain_row
    return inverse * (scaled - unit_rows * jnp.mean(scaled * unit_rows, axis=-1, keepdims=True))


def silu_parts(values):
    sigma = jax.nn.sigmoid(values)
    return (values * sigma, sigma * (1.0 + values * (1.0 - sigma)))


def dot(left, right):
    return jnp.dot(left, right, preferred_element_type=F32)


def dot_nt(left, right):
    return lax.dot_general(left, right, (((1,), (1,)), ((), ())), preferred_element_type=F32)


def dot_tn(left, right):
    return lax.dot_general(left, right, (((0,), (0,)), ((), ())), preferred_element_type=F32)


def attention_scores(query_rot, key_rot, allowed):
    scores = jnp.einsum("qhd,khd->hqk", query_rot, key_rot, preferred_element_type=F32)
    return jnp.where(allowed[None], scores * HD ** (-0.5), MASKED_SCORE)


def make_body(dp):
    outer, inner = split_dp(dp)

    def attn_forward(x_rows, gain, w_attn, allowed, cosine, sine):
        heads_width = w_attn.shape[1] // 4
        unit, inverse = normed(x_rows)
        a_in = gather((unit * gain).astype(BF16), 1, dp, 0).reshape(-1, x_rows.shape[1])
        count = a_in.shape[0]
        raw = dot(a_in, w_attn[:, : 3 * heads_width])
        query = raw[:, :heads_width].reshape(count, -1, HD)
        key_raw = raw[:, heads_width : 2 * heads_width].reshape(count, -1, HD)
        value = raw[:, 2 * heads_width :].astype(BF16).reshape(count, -1, HD)
        query_rot = rotate(query, cosine, sine).astype(BF16)
        key_rot = rotate(key_raw, cosine, sine).astype(BF16)
        scores = attention_scores(query_rot, key_rot, allowed)
        top_score = jnp.max(scores, axis=-1, keepdims=True)
        expo = jnp.exp(scores - top_score)
        total = jnp.sum(expo, axis=-1, keepdims=True)
        probs = (expo / total).astype(BF16)
        log_total = top_score + jnp.log(total)
        attended = (
            jnp.einsum("hqk,khd->qhd", probs, value, preferred_element_type=F32)
            .astype(BF16)
            .reshape(count, heads_width)
        )
        part = dot_nt(attended, w_attn[:, 3 * heads_width :]).astype(BF16)
        resid = x_rows + scatter(part.reshape((1, 2, 2) + x_rows.shape), 1, dp, 1)
        return resid, (unit, inverse, a_in, query_rot, key_rot, value, log_total, attended)

    def ffn_forward(resid, gain, w_ffn, mixing):
        third = w_ffn.shape[1] // 3
        unit, inverse = normed(resid)
        b_in = gather((unit * gain).astype(BF16), outer, inner, 2).reshape(-1, resid.shape[1])
        both = dot(b_in, w_ffn[:, : 2 * third])
        gate, up = both[:, :third], both[:, third:]
        hidden = (mixing * jax.nn.silu(gate) * up).astype(BF16)
        part = dot_nt(hidden, w_ffn[:, 2 * third :]).astype(BF16)
        output = resid + scatter(part.reshape((outer, 2, 2) + resid.shape), outer, inner, 3)
        return output, (unit, inverse, b_in, both.astype(BF16), hidden)

    def ffn_backward(grad_y, kept, gain, w_ffn, mixing):
        unit, inverse, b_in, both, hidden = kept
        third = w_ffn.shape[1] // 3
        width = grad_y.shape[1]
        grad_branch = gather(grad_y.astype(BF16), outer, inner, 2).reshape(-1, width)
        grad_down = dot_tn(grad_branch, hidden).astype(BF16)
        gate, up = both[:, :third].astype(F32), both[:, third:].astype(F32)
        grad_hidden = dot(grad_branch, w_ffn[:, 2 * third :]) * mixing
        act, slope = silu_parts(gate)
        grad_both = jnp.concatenate(
            [(grad_hidden * up * slope).astype(BF16), (grad_hidden * act).astype(BF16)], axis=1
        )
        part = dot_nt(grad_both, w_ffn[:, : 2 * third]).astype(BF16)
        grad_b = scatter(part.reshape((outer, 2, 2) + grad_y.shape), outer, inner, 3)
        grad_in = dot_tn(b_in, grad_both).astype(BF16)
        part_gain = jnp.sum(grad_b * unit, axis=0)
        grad_resid = grad_y + norm_back(grad_b, gain, unit, inverse)
        return grad_resid, part_gain, grad_in, grad_down

    def attn_backward(grad_resid, kept, gain, w_attn, allowed, cosine, sine):
        unit, inverse, a_in, query_rot, key_rot, value, log_total, attended = kept
        heads_width = w_attn.shape[1] // 4
        width = grad_resid.shape[1]
        grad_attn = gather(grad_resid.astype(BF16), 1, dp, 0).reshape(-1, width)
        count = grad_attn.shape[0]
        grad_out = dot_tn(grad_attn, attended).astype(BF16)
        grad_attended = (
            dot(grad_attn, w_attn[:, 3 * heads_width :]).astype(BF16).reshape(count, -1, HD)
        )
        scores = attention_scores(query_rot, key_rot, allowed)
        probs_full = jnp.exp(scores - log_total)
        probs = probs_full.astype(BF16)
        grad_value = (
            jnp.einsum("hqk,qhd->khd", probs, grad_attended, preferred_element_type=F32)
            .astype(BF16)
            .reshape(count, heads_width)
        )
        grad_probs = jnp.einsum("qhd,khd->hqk", grad_attended, value, preferred_element_type=F32)
        grad_scores = (
            probs_full * (grad_probs - jnp.sum(grad_probs * probs_full, axis=-1, keepdims=True))
        ).astype(BF16)
        grad_qrot = jnp.einsum(
            "hqk,khd->qhd", grad_scores, key_rot, preferred_element_type=F32
        ) * HD ** (-0.5)
        grad_krot = jnp.einsum(
            "hqk,qhd->khd", grad_scores, query_rot, preferred_element_type=F32
        ) * HD ** (-0.5)
        grad_query = rotate(grad_qrot, cosine, -sine).astype(BF16).reshape(count, heads_width)
        grad_key = rotate(grad_krot, cosine, -sine).astype(BF16).reshape(count, heads_width)
        grad_raw = jnp.concatenate([grad_query, grad_key, grad_value], axis=1)
        part = dot_nt(grad_raw, w_attn[:, : 3 * heads_width]).astype(BF16)
        grad_a = scatter(part.reshape((1, 2, 2) + grad_resid.shape), 1, dp, 1)
        grad_raw_w = dot_tn(a_in, grad_raw).astype(BF16)
        part_gain = jnp.sum(grad_a * unit, axis=0)
        grad_x = grad_resid + norm_back(grad_a, gain, unit, inverse)
        return grad_x, part_gain, jnp.concatenate([grad_raw_w, grad_out], axis=1)

    def body(
        tokens,
        place,
        lengths,
        expert_ids,
        gate_values,
        cotangent,
        gain_attn,
        w_query,
        w_key,
        w_value,
        w_out,
        gain_ffn,
        exp_gate,
        exp_up,
        exp_down,
        dense_gate,
        dense_up,
        dense_down,
    ):
        layers, experts, rows, full = exp_gate.shape
        width = tokens.shape[1]
        slim = full // outer
        count = place.shape[1]
        segment, position = layout(place[0], lengths[0])
        allowed = (segment[:, None] == segment[None, :]) & (
            position[None, :] <= position[:, None]
        )
        cosine, sine = rope_tables(position, HD)

        slots = expert_ids[:, None] == jnp.arange(experts, dtype=jnp.int32)[None, :, None, None]
        mix_own = jnp.sum(jnp.where(slots, gate_values[:, None], 0.0), axis=-1)
        gains_own = jnp.pad(
            jnp.concatenate([gain_attn, gain_ffn], axis=0).astype(BF16).astype(F32),
            ((0, 8 - 2 * layers), (0, count - rows)),
        )
        small_own = jnp.concatenate([mix_own.reshape(-1, count), gains_own], axis=0)

        attn_own, ffn_own = [], []
        for level in range(layers):
            attn_own.append(
                jnp.concatenate(
                    [w_query[level], w_key[level], w_value[level], jnp.transpose(w_out[level])],
                    axis=1,
                ).astype(BF16)[None]
            )
            mats = (
                [exp_gate[level, e] for e in range(experts)]
                + [dense_gate[level]]
                + [exp_up[level, e] for e in range(experts)]
                + [dense_up[level]]
                + [jnp.transpose(exp_down[level, e]) for e in range(experts)]
                + [jnp.transpose(dense_down[level])]
            )
            mats = [m.astype(BF16) for m in mats]
            ffn_own.append(
                jnp.stack(
                    [
                        jnp.concatenate([m[:, k * slim : (k + 1) * slim] for m in mats], axis=1)
                        for k in range(outer)
                    ]
                )
            )
        first = fetch([small_own[None], attn_own[0], ffn_own[0]], outer, inner, 4)
        small_all = first[0]
        fetched = [first[1:]]
        for level in range(1, layers):
            fetched.append(fetch([attn_own[level], ffn_own[level]], outer, inner, 5))
        w_attn = [pair[0].reshape(width, -1) for pair in fetched]
        w_ffn = [pair[1].reshape(width, -1) for pair in fetched]

        gains = jnp.transpose(small_all[:, layers * experts :, :rows], (1, 0, 2)).reshape(8, width)
        dx = lax.rem(lax.axis_index("dp"), inner)
        mix_all = lax.dynamic_index_in_dim(
            small_all[:, : layers * experts].reshape(outer, inner, layers, experts, count),
            dx,
            axis=1,
            keepdims=False,
        )
        mixing = []
        for level in range(layers):
            mix_rows = jnp.transpose(mix_all[:, level], (0, 2, 1)).reshape(outer * count, experts)
            mixing.append(
                jnp.concatenate(
                    [
                        jnp.broadcast_to(mix_rows[:, e : e + 1], (outer * count, slim))
                        for e in range(experts)
                    ]
                    + [jnp.ones((outer * count, slim), F32)],
                    axis=1,
                )
            )

        state = tokens.astype(F32)
        kept_attn, kept_ffn = [], []
        for level in range(layers):
            state, kept = attn_forward(
                state, gains[level][None], w_attn[level], allowed, cosine, sine
            )
            kept_attn.append(kept)
            state, kept = ffn_forward(
                state, gains[layers + level][None], w_ffn[level], mixing[level]
            )
            kept_ffn.append(kept)
        mixed = state.astype(BF16)

        grad = cotangent.astype(F32)
        part_gains = [None] * (2 * layers)
        pushed = [None] * layers
        for level in reversed(range(layers)):
            grad, part_gains[layers + level], grad_in, grad_down = ffn_backward(
                grad, kept_ffn[level], gains[layers + level][None], w_ffn[level], mixing[level]
            )
            grad, part_gains[level], grad_attn = attn_backward(
                grad,
                kept_attn[level],
                gains[level][None],
                w_attn[level],
                allowed,
                cosine,
                sine,
            )
            parts = [
                grad_in.reshape(dp, rows, -1),
                grad_down.reshape(dp, rows, -1),
                grad_attn.reshape(dp, rows, -1),
            ]
            if level == 0:
                stacked = jnp.pad(jnp.stack(part_gains), ((0, 8 - 2 * layers), (0, 0)))
                parts.append(jnp.transpose(stacked.reshape(8, dp, rows), (1, 0, 2)))
                pushed[level] = push(parts, outer, inner, 6)
            else:
                pushed[level] = push(parts, outer, inner, 7)

        gain_part = jnp.sum(pushed[0][3], axis=0)
        gain_sum = jnp.sum(
            gather(jnp.pad(gain_part, ((0, 0), (0, 128 - rows))), 1, dp, 8)[0], axis=0
        )
        grad_gain_attn = gain_sum[:layers, :rows]
        grad_gain_ffn = gain_sum[layers : 2 * layers, :rows]

        kinds = experts + 1
        ups, downs, attns = [], [], []
        for level in range(layers):
            in_part, down_part, attn_part = pushed[level][:3]
            ups.append(
                jnp.concatenate(
                    [
                        jnp.stack(
                            [
                                in_part[k][:, m * slim : (m + 1) * slim]
                                for m in range(2 * kinds)
                            ]
                        )
                        for k in range(outer)
                    ],
                    axis=2,
                )
            )
            downs.append(
                jnp.concatenate(
                    [
                        jnp.stack(
                            [
                                jnp.transpose(down_part[k][:, m * slim : (m + 1) * slim])
                                for m in range(kinds)
                            ]
                        )
                        for k in range(outer)
                    ],
                    axis=1,
                )
            )
            attns.append(jnp.sum(attn_part.astype(F32), axis=0))
        up = jnp.stack(ups).astype(F32)
        down = jnp.stack(downs).astype(F32)
        attn = jnp.stack(attns)
        quarter = attn.shape[-1] // 4
        return (
            mixed,
            grad,
            grad_gain_attn,
            attn[:, :, :quarter],
            attn[:, :, quarter : 2 * quarter],
            attn[:, :, 2 * quarter : 3 * quarter],
            jnp.swapaxes(attn[:, :, 3 * quarter :], 1, 2),
            grad_gain_ffn,
            up[:, :experts],
            up[:, kinds : kinds + experts],
            down[:, :experts],
            up[:, experts],
            up[:, kinds + experts],
            down[:, experts],
        )

    return body


def solution(mesh):
    return jax.shard_map(
        make_body(mesh.shape["dp"]),
        mesh=mesh,
        in_specs=(
            P(("dp", "tensor"), None),
            P("dp", None),
            P("dp", None),
            P(None, "dp", None),
            P(None, "dp", None),
            P(("dp", "tensor"), None),
            P(None, "dp"),
            P(None, "dp", "tensor"),
            P(None, "dp", "tensor"),
            P(None, "dp", "tensor"),
            P(None, "tensor", "dp"),
            P(None, "dp"),
            P(None, None, "dp", "tensor"),
            P(None, None, "dp", "tensor"),
            P(None, None, "tensor", "dp"),
            P(None, "dp", "tensor"),
            P(None, "dp", "tensor"),
            P(None, "tensor", "dp"),
        ),
        out_specs=(
            P(("dp", "tensor"), None),
            P(("dp", "tensor"), None),
            P(None, "dp"),
            P(None, "dp", "tensor"),
            P(None, "dp", "tensor"),
            P(None, "dp", "tensor"),
            P(None, "tensor", "dp"),
            P(None, "dp"),
            P(None, None, "dp", "tensor"),
            P(None, None, "dp", "tensor"),
            P(None, None, "tensor", "dp"),
            P(None, "dp", "tensor"),
            P(None, "dp", "tensor"),
            P(None, "tensor", "dp"),
        ),
        check_vma=False,
    )
```

time: 2580 us -> 835 us (0.32)
  waiting for transfers between devices: 1640 us -> 0 us
  blocking collectives: 605 us -> 0 us
  Pallas kernels: 0 us -> 595 us
  matrix products: 163 us -> 112 us
    reduce_scatter x22 -> x0, waiting for transfers between devices: 1580 us -> none  [the longest x2 370 us: sum_layer(): lax.psum_scatter(grads[1], 'dp', scatter_dimension=0, tiled=True)]
    pallas_call x0 -> x21, Pallas kernels: none -> 595 us  [the longest x8 184 us: scatter(): pl.pallas_call(functools.partial(scatter_kernel, outer, inner), out_shape...]
    all_gather x22 -> x0, blocking collectives: 549 us -> none  [the longest x4 118 us: gather_normed(): return lax.all_gather(rows, 'tensor', axis=0, tiled=True)]
    all_gather x6 -> x0, waiting for transfers between devices: 57.6 us -> none  [the longest x2 56.4 us: fetch_weights(): lax.all_gather(shards[7], 'dp', axis=1, tiled=True)]
    dot_general x70 -> x36, matrix products: 158 us -> 112 us  [the longest x8 42.5 us: dot(): return jnp.dot(left, right, preferred_element_type=F32)]
    unnamed x2 -> x0, blocking collectives: 43.5 us -> none
    transpose x4 -> x1, local copies, waits for them, and re-layouts: 31.4 us -> 0.79 us  [body(): jnp.transpose(small_all[:, layers * experts:, :rows], (1, 0, 2))]
  transfers between devices with their start and end apart: 31 -> 0, of which waited for: 22 -> 0; matrix products, arithmetic and copies ran while one was open for 8% -> 0% of each run, Pallas kernels for 0% -> 0%
where the time goes in v1:
time: 835 us; the launch traced here: 819 us
  Pallas kernels  595 us (71%)
  matrix products  112 us (13%)
  local copies, waits for them, and re-layouts  58.3 us (7%)
  other arithmetic  51.1 us (6%)
    pallas_call x8, Pallas kernels, scatter(): pl.pallas_call(functools.partial(scatter_kernel, outer, inner), out_shape...  184 us
    pallas_call x9, Pallas kernels, gather(): pl.pallas_call(functools.partial(gather_kernel, outer, inner), out_shape=...  169 us
    pallas_call x2, Pallas kernels, fetch(): pl.pallas_call(functools.partial(fetch_kernel, outer, inner, count), out_...  123 us
    pallas_call x2, Pallas kernels, push(): pl.pallas_call(functools.partial(push_kernel, outer, inner, count), out_s...  119 us
    dot_general x8, matrix products, dot(): return jnp.dot(left, right, preferred_element_type=F32)  42.5 us
    unnamed x351, local copies, waits for them, and re-layouts  34.5 us
    dot_general x8, matrix products, dot_nt(): lax.dot_general(left, right, (((1,), (1,)), ((), ())), preferred_element_...  32.4 us
    dot_general x8, matrix products, dot_tn(): lax.dot_general(left, right, (((0,), (0,)), ((), ())), preferred_element_...  26.2 us

profile of v1, /device:TPU:9, one launch (start us, length us, event | category | flops | bytes accessed | tf_op | source)
XLA Modules:
  0.0 819.2 jit_solution(16315756106462317491)
XLA Ops:
  12.7 64.0 %fetch.2 = (f32[8,16,512]{2,1,0:T(8,128)}, bf16[8,96,768]{2,1,0:T(8,128)(2,1)}, bf16[8,96,1920]{2,1,0:T(8,128)(2,1)}) custom-call(f32[1,16,512]{2,1,0:T(8,128)} %maximum_bitcast_fusion.4.refs_0_, bf16[1,96,768]{2,1,0:T(8,128)(2,1)} %get-tuple-element.362.refs_1_, bf16[4,96,1920]{2,1,0:T(8,128)(2,1)} %pad_maximum_fusion.6.refs_2_), custom_call_target="tpu_custom_call" | custom-call | tf_op jit(solution)/shard_map/fetch/pallas_call | solution.py:229
  91.1 11.2 %gather.9 = bf16[1,4,128,768]{3,2,1,0:T(8,128)(2,1)} custom-call(bf16[128,768]{1,0:T(8,128)(2,1)} %fusion.65.own), custom_call_target="tpu_custom_call" | custom-call | tf_op jit(solution)/shard_map/gather/pallas_call | solution.py:93
  111.2 2.4 convolution_convert_fusion.13
  113.6 10.4 %scatter.8 = f32[128,768]{1,0:T(8,128)} custom-call(bf16[1,2,2,128,768]{4,3,2,1,0:T(8,128)(2,1)} %bitcast.860), custom_call_target="tpu_custom_call" | custom-call | tf_op jit(solution)/shard_map/scatter/pallas_call | solution.py:162
  127.2 32.5 %gather.10 = bf16[4,4,128,768]{3,2,1,0:T(8,128)(2,1)} custom-call(bf16[128,768]{1,0:T(8,128)(2,1)} %multiply_convert_fusion.4.own), custom_call_target="tpu_custom_call" | custom-call | tf_op jit(solution)/shard_map/gather/pallas_call | solution.py:93
  159.7 9.3 %fusion.121 = (bf16[2048,1280]{0,1:T(8,128)(2,1)}, f32[2048,1280]{0,1:T(8,128)S(1)}) fusion(bf16[2048,768]{1,0:T(8,128)(2,1)} %bitcast.848, bf16[768,1920]{1,0:T(8,128)(2,1)} %bitcast.935), kind=kOutput, calls=%fused_computation.683 | convolution fusion | flops 4029153280 | bytes 20840448 | tf_op jit(solution)/shard_map/dot_general | solution.py:355
  169.1 3.6 fusion.19
  172.7 6.1 convolution_convert_fusion.1
  178.8 35.3 %scatter.9 = f32[128,768]{1,0:T(8,128)} custom-call(bf16[4,2,2,128,768]{4,3,2,1,0:T(8,128)(2,1)} %bitcast.858), custom_call_target="tpu_custom_call" | custom-call | tf_op jit(solution)/shard_map/scatter/pallas_call | solution.py:162
  217.8 10.1 %gather.11 = bf16[1,4,128,768]{3,2,1,0:T(8,128)(2,1)} custom-call(bf16[128,768]{1,0:T(8,128)(2,1)} %multiply_convert_fusion.3.own), custom_call_target="tpu_custom_call" | custom-call | tf_op jit(solution)/shard_map/gather/pallas_call | solution.py:93
  243.6 2.6 pad_maximum_fusion.7.refs_1_
  246.3 58.9 %fetch.3 = (bf16[8,96,768]{2,1,0:T(8,128)(2,1)}, bf16[8,96,1920]{2,1,0:T(8,128)(2,1)}) custom-call(bf16[1,96,768]{2,1,0:T(8,128)(2,1)} %get-tuple-element.363.refs_0_, bf16[4,96,1920]{2,1,0:T(8,128)(2,1)} %pad_maximum_fusion.7.refs_1_), custom_call_target="tpu_custom_call" | custom-call | tf_op jit(solution)/shard_map/fetch/pallas_call | solution.py:229
  305.2 2.2 fusion.54
  311.4 2.4 convolution_convert_fusion.12
  313.9 12.0 %scatter.10 = f32[128,768]{1,0:T(8,128)} custom-call(bf16[1,2,2,128,768]{4,3,2,1,0:T(8,128)(2,1)} %bitcast.861), custom_call_target="tpu_custom_call" | custom-call | tf_op jit(solution)/shard_map/scatter/pallas_call | solution.py:162
  325.9 1.9 multiply_reduce_fusion.8
  329.6 33.4 %gather.12 = bf16[4,4,128,768]{3,2,1,0:T(8,128)(2,1)} custom-call(bf16[128,768]{1,0:T(8,128)(2,1)} %multiply_convert_fusion.2.own), custom_call_target="tpu_custom_call" | custom-call | tf_op jit(solution)/shard_map/gather/pallas_call | solution.py:93
  363.1 9.1 %fusion.120 = (bf16[2048,1280]{0,1:T(8,128)(2,1)}, f32[2048,1280]{0,1:T(8,128)S(1)}) fusion(bf16[2048,768]{1,0:T(8,128)(2,1)} %bitcast.850, bf16[768,1920]{1,0:T(8,128)(2,1)} %bitcast.939), kind=kOutput, calls=%fused_computation.682 | convolution fusion | flops 4029153280 | bytes 20840448 | tf_op jit(solution)/shard_map/dot_general | solution.py:355
  372.2 3.6 fusion.18
  375.8 6.2 convolution_convert_fusion
  382.0 36.0 %scatter.11 = f32[128,768]{1,0:T(8,128)} custom-call(bf16[4,2,2,128,768]{4,3,2,1,0:T(8,128)(2,1)} %bitcast.859), custom_call_target="tpu_custom_call" | custom-call | tf_op jit(solution)/shard_map/scatter/pallas_call | solution.py:162
  418.7 28.0 %gather.13 = bf16[4,4,128,768]{3,2,1,0:T(8,128)(2,1)} custom-call(bf16[128,768]{1,0:T(8,128)(2,1)} %own), custom_call_target="tpu_custom_call" | custom-call | tf_op jit(solution)/shard_map/gather/pallas_call | solution.py:93
  446.7 8.1 fusion.6
  454.9 6.0 convolution_convert_fusion.5
  460.9 34.3 %scatter.12 = f32[128,768]{1,0:T(8,128)} custom-call(bf16[4,2,2,128,768]{4,3,2,1,0:T(8,128)(2,1)} %bitcast.856), custom_call_target="tpu_custom_call" | custom-call | tf_op jit(solution)/shard_map/scatter/pallas_call | solution.py:162
  495.2 1.9 multiply_reduce_fusion.2
  497.8 2.0 fusion.104.own
  499.8 9.7 %gather.14 = bf16[1,4,128,768]{3,2,1,0:T(8,128)(2,1)} custom-call(bf16[128,768]{1,0:T(8,128)(2,1)} %fusion.104.own), custom_call_target="tpu_custom_call" | custom-call | tf_op jit(solution)/shard_map/gather/pallas_call | solution.py:93
  511.3 2.8 multiply_reduce_fusion.1
  519.3 10.4 %scatter.13 = f32[128,768]{1,0:T(8,128)} custom-call(bf16[1,2,2,128,768]{4,3,2,1,0:T(8,128)(2,1)} %bitcast.891), custom_call_target="tpu_custom_call" | custom-call | tf_op jit(solution)/shard_map/scatter/pallas_call | solution.py:162
  529.7 1.9 multiply_reduce_fusion.4
  531.7 2.7 fusion.106
  534.3 28.4 %gather.15 = bf16[4,4,128,768]{3,2,1,0:T(8,128)(2,1)} custom-call(bf16[128,768]{1,0:T(8,128)(2,1)} %get-tuple-element.110.own), custom_call_target="tpu_custom_call" | custom-call | tf_op jit(solution)/shard_map/gather/pallas_call | solution.py:93
  562.8 8.4 %fusion.15 = (bf16[2048,640]{0,1:T(8,128)(2,1)S(1)}, bf16[2048,640]{0,1:T(8,128)(2,1)S(1)}) fusion(bf16[2048,1280]{0,1:T(8,128)(2,1)} %get-tuple-element.358, f32[2048,640]{0,1:T(8,128)} %broadcast_dynamic-update-slice_fusion.5, bf16[2048,768]{1,0:T(8,128)(2,1)} %bitcast.854, bf16[768,1920]{1,0:T(8,128)(2,1)} %bitcast.937), kind=kOutput, calls=%fused_computation.21 | convolution fusion | flops 2034237440 | bytes 19857408 | tf_op jit(solution)/shard_map/dot_general | solution.py:355
  571.1 5.9 convolution_convert_fusion.4
  577.1 35.3 %scatter.14 = f32[128,768]{1,0:T(8,128)} custom-call(bf16[4,2,2,128,768]{4,3,2,1,0:T(8,128)(2,1)} %bitcast.857), custom_call_target="tpu_custom_call" | custom-call | tf_op jit(solution)/shard_map/scatter/pallas_call | solution.py:162
  614.2 2.1 fusion.105
  616.3 9.7 %gather.16 = bf16[1,4,128,768]{3,2,1,0:T(8,128)(2,1)} custom-call(bf16[128,768]{1,0:T(8,128)(2,1)} %get-tuple-element.108.own), custom_call_target="tpu_custom_call" | custom-call | tf_op jit(solution)/shard_map/gather/pallas_call | solution.py:93
  635.2 10.5 %scatter.15 = f32[128,768]{1,0:T(8,128)} custom-call(bf16[1,2,2,128,768]{4,3,2,1,0:T(8,128)(2,1)} %bitcast.892), custom_call_target="tpu_custom_call" | custom-call | tf_op jit(solution)/shard_map/scatter/pallas_call | solution.py:162
  649.7 1.8 copy.95
  651.6 6.4 convolution_convert_fusion.7
  658.0 5.6 convolution_convert_fusion.3
  663.6 60.0 %push.2 = (bf16[4,96,1280]{2,1,0:T(8,128)(2,1)}, bf16[4,96,640]{2,1,0:T(8,128)(2,1)}, bf16[4,96,768]{2,1,0:T(8,128)(2,1)}, f32[4,8,96]{2,1,0:T(8,128)}) custom-call(bf16[8,96,1280]{2,1,0:T(8,128)(2,1)} %bitcast.875, bf16[8,96,640]{2,1,0:T(8,128)(2,1)} %bitcast.886, bf16[8,96,768]{2,1,0:T(8,128)(2,1)} %bitcast.845, f32[8,8,96]{2,1,0:T(8,128)} %bitcast.917), custom_call_target="tpu_custom_call" | custom-call | tf_op jit(solution)/shard_map/push/pallas_call | solution.py:296
  727.9 9.2 %convolution_convert_fusion.2 = bf16[768,1280]{1,0:T(8,128)(2,1)} fusion(bf16[2048,768]{1,0:T(8,128)(2,1)} %bitcast.851, bf16[2048,640]{0,1:T(8,128)(2,1)} %copy-done.100, bf16[2048,640]{0,1:T(8,128)(2,1)} %copy-done.99), kind=kOutput, calls=%fused_computation.34 | convolution fusion | flops 4038000640 | bytes 10354688 | tf_op jit(solution)/shard_map/dot_general | solution.py:363
  737.1 2.2 fusion.38
  740.6 58.7 %push.3 = (bf16[4,96,1280]{2,1,0:T(8,128)(2,1)}, bf16[4,96,640]{2,1,0:T(8,128)(2,1)}, bf16[4,96,768]{2,1,0:T(8,128)(2,1)}) custom-call(bf16[8,96,1280]{2,1,0:T(8,128)(2,1)} %bitcast.874, bf16[8,96,640]{2,1,0:T(8,128)(2,1)} %bitcast.847, bf16[8,96,768]{2,1,0:T(8,128)(2,1)} %bitcast.846), custom_call_target="tpu_custom_call" | custom-call | tf_op jit(solution)/shard_map/push/pallas_call | solution.py:296
  806.3 2.0 fusion.108
  810.8 6.0 gather.17
  (504 shorter events, 102.5 us)
Async XLA Ops:
  0.6 4.5 copy-start.55
  0.7 5.2 copy-start.22
  7.8 3.1 copy-start.63
  8.8 3.2 copy-start.86
  8.8 3.2 copy-start.87
  8.9 3.2 copy-start.97
  8.9 3.2 copy-start.98
  82.1 8.1 copy-start.4
  84.4 18.0 %copy-start.12 = (bf16[8,96,768]{2,1,0:T(8,128)(2,1)S(1)}, bf16[8,96,768]{2,1,0:T(8,128)(2,1)}, u32[]{:S(2)}) copy-start(bf16[8,96,768]{2,1,0:T(8,128)(2,1)} %get-tuple-element.27) | copy-start | bytes 3538948
  88.7 16.6 %copy-start.94 = (s32[1,3]{1,0:T(1,128)S(1)}, s32[1,3]{1,0:T(1,128)}, u32[]{:S(2)}) copy-start(s32[1,3]{1,0:T(1,128)} %param.20) | copy-start | bytes 40
  88.7 16.7 %copy-start.80 = (s32[1,512]{1,0:T(1,128)S(1)}, s32[1,512]{1,0:T(1,128)}, u32[]{:S(2)}) copy-start(s32[1,512]{1,0:T(1,128)} %param.19) | copy-start | bytes 6148
  90.3 16.3 %copy-start.90 = (f32[128]{0:T(128)}, f32[128]{0:T(128)S(1)}, u32[]{:S(2)}) copy-start(f32[128]{0:T(128)S(1)} %add_rsqrt_fusion.3) | copy-start | bytes 1540
  125.8 43.3 %copy-start.71 = (f32[768]{0:T(1024)}, f32[768]{0:T(1024)S(1)}, u32[]{:S(2)}) copy-start(f32[768]{0:T(1024)S(1)} %mul.537) | copy-start | bytes 9220
  172.7 6.1 copy-start.15
  216.0 30.3 %copy-start.92 = (f32[128]{0:T(128)}, f32[128]{0:T(128)S(1)}, u32[]{:S(2)}) copy-start(f32[128]{0:T(128)S(1)} %add_rsqrt_fusion.1) | copy-start | bytes 1540
  216.0 30.2 %copy-start.73 = (f32[768]{0:T(1024)}, f32[768]{0:T(1024)S(1)}, u32[]{:S(2)}) copy-start(f32[768]{0:T(1024)S(1)} %mul.546) | copy-start | bytes 9220
  311.4 16.3 %copy-start.85 = (f32[8,96]{1,0:T(8,128)S(1)}, f32[8,96]{1,0:T(8,128)}, u32[]{:S(2)}) copy-start(f32[8,96]{1,0:T(8,128)} %get-tuple-element.102) | copy-start | bytes 9220
  327.8 44.4 %copy-start.88 = (f32[128]{0:T(128)}, f32[128]{0:T(128)S(1)}, u32[]{:S(2)}) copy-start(f32[128]{0:T(128)S(1)} %add_rsqrt_fusion) | copy-start | bytes 1540
  375.8 6.2 copy-start.16
  446.7 8.2 copy-start.96
  454.9 6.0 copy-start.99
  454.9 6.0 copy-start.100
  517.0 12.7 %copy-start.74 = (f32[768]{0:T(1024)S(1)}, f32[768]{0:T(1024)}, u32[]{:S(2)}) copy-start(f32[768]{0:T(1024)} %copy-done.73) | copy-start | bytes 9220
  517.1 14.6 %copy-start.89 = (f32[128]{0:T(128)S(1)}, f32[128]{0:T(128)}, u32[]{:S(2)}) copy-start(f32[128]{0:T(128)} %copy-done.88) | copy-start | bytes 1540
  562.7 8.4 %copy-start.95 = (bf16[8,96,1920]{2,1,0:T(8,128)(2,1)S(1)}, bf16[8,96,1920]{2,1,0:T(8,128)(2,1)}, u32[]{:S(2)}) copy-start(bf16[8,96,1920]{2,1,0:T(8,128)(2,1)} %get-tuple-element.28) | copy-start | bytes 8847364
  571.1 6.0 copy-start.101
  571.1 6.0 copy-start.103
  577.1 35.3 %copy-start.72 = (f32[768]{0:T(1024)S(1)}, f32[768]{0:T(1024)}, u32[]{:S(2)}) copy-start(f32[768]{0:T(1024)} %copy-done.71) | copy-start | bytes 9220
  612.4 15.4 %copy-start.76 = (f32[3,512]{1,0:T(4,128)S(1)}, f32[3,512]{1,0:T(4,128)}, u32[]{:S(2)}) copy-start(f32[3,512]{1,0:T(4,128)} %copy-done.75) | copy-start | bytes 18436
  632.9 12.7 %copy-start.5 = (bf16[128,768]{1,0:T(8,128)(2,1)S(1)}, bf16[128,768]{1,0:T(8,128)(2,1)}, u32[]{:S(2)}) copy-start(bf16[128,768]{1,0:T(8,128)(2,1)} %param.18) | copy-start | bytes 589828
  632.9 12.7 %copy-start.91 = (f32[128]{0:T(128)S(1)}, f32[128]{0:T(128)}, u32[]{:S(2)}) copy-start(f32[128]{0:T(128)} %copy-done.90) | copy-start | bytes 1540
  632.9 14.0 %copy-start.83 = (f32[768]{0:T(1024)S(1)}, f32[768]{0:T(1024)}, u32[]{:S(2)}) copy-start(f32[768]{0:T(1024)} %get-tuple-element.96) | copy-start | bytes 9220
  633.0 14.0 %copy-start.82 = (f32[768]{0:T(1024)S(1)}, f32[768]{0:T(1024)}, u32[]{:S(2)}) copy-start(f32[768]{0:T(1024)} %get-tuple-element.94) | copy-start | bytes 9220
  633.0 14.0 %copy-start.81 = (f32[768]{0:T(1024)S(1)}, f32[768]{0:T(1024)}, u32[]{:S(2)}) copy-start(f32[768]{0:T(1024)} %get-tuple-element.98) | copy-start | bytes 9220
  633.0 14.7 %copy-start.10 = (bf16[1,4,128,768]{3,2,1,0:T(8,128)(2,1)S(1)}, bf16[1,4,128,768]{3,2,1,0:T(8,128)(2,1)}, u32[]{:S(2)}) copy-start(bf16[1,4,128,768]{3,2,1,0:T(8,128)(2,1)} %gather.9) | copy-start | bytes 2359300
  635.2 14.1 %copy-start.3 = (bf16[1,4,128,768]{3,2,1,0:T(8,128)(2,1)S(1)}, bf16[1,4,128,768]{3,2,1,0:T(8,128)(2,1)}, u32[]{:S(2)}) copy-start(bf16[1,4,128,768]{3,2,1,0:T(8,128)(2,1)} %gather.16) | copy-start | bytes 2359300
  635.2 14.1 %copy-start.30 = (bf16[3,64,512]{2,1,0:T(8,128)(2,1)S(1)}, bf16[3,64,512]{2,1,0:T(8,128)(2,1)}, u32[]{:S(2)}) copy-start(bf16[3,64,512]{2,1,0:T(8,128)(2,1)} %copy-done.29) | copy-start | bytes 589828
  651.6 6.5 copy-start.8
  651.6 6.5 copy-start.102
  651.6 6.4 copy-start.104
  663.6 61.6 %copy-start.11 = (bf16[1,4,128,768]{3,2,1,0:T(8,128)(2,1)S(1)}, bf16[1,4,128,768]{3,2,1,0:T(8,128)(2,1)}, u32[]{:S(2)}) copy-start(bf16[1,4,128,768]{3,2,1,0:T(8,128)(2,1)} %gather.11) | copy-start | bytes 2359300
  663.6 61.6 %copy-start.61 = (bf16[3,64,512]{2,1,0:T(8,128)(2,1)S(1)}, bf16[3,64,512]{2,1,0:T(8,128)(2,1)}, u32[]{:S(2)}) copy-start(bf16[3,64,512]{2,1,0:T(8,128)(2,1)} %copy-done.60) | copy-start | bytes 589828
  663.6 61.6 %copy-start.67 = (bf16[512,3,64]{0,2,1:T(8,128)(2,1)S(1)}, bf16[512,3,64]{0,2,1:T(8,128)(2,1)}, u32[]{:S(2)}) copy-start(bf16[512,3,64]{0,2,1:T(8,128)(2,1)} %copy-done.66) | copy-start | bytes 589828
  663.6 61.6 %copy-start.69 = (bf16[512,3,64]{0,2,1:T(8,128)(2,1)S(1)}, bf16[512,3,64]{0,2,1:T(8,128)(2,1)}, u32[]{:S(2)}) copy-start(bf16[512,3,64]{0,2,1:T(8,128)(2,1)} %copy-done.68) | copy-start | bytes 589828
  727.9 9.2 %copy-start.9 = (bf16[4,4,128,768]{3,2,1,0:T(8,128)(2,1)S(1)}, bf16[4,4,128,768]{3,2,1,0:T(8,128)(2,1)}, u32[]{:S(2)}) copy-start(bf16[4,4,128,768]{3,2,1,0:T(8,128)(2,1)} %gather.13) | copy-start | bytes 9437188
  727.9 9.2 %copy-start.17 = (bf16[2048,640]{0,1:T(8,128)(2,1)S(1)}, bf16[2048,640]{0,1:T(8,128)(2,1)}, u32[]{:S(2)}) copy-start(bf16[2048,640]{0,1:T(8,128)(2,1)} %copy-done.16) | copy-start | bytes 7864324
  808.3 9.8 %copy-start.7 = (f32[128,768]{1,0:T(8,128)S(1)}, f32[128,768]{1,0:T(8,128)}, u32[]{:S(2)}) copy-start(f32[128,768]{1,0:T(8,128)} %scatter.15) | copy-start | bytes 1179652
  808.3 9.8 %copy-start.24 = (f32[128,768]{1,0:T(8,128)S(1)}, f32[128,768]{1,0:T(8,128)}, u32[]{:S(2)}) copy-start(f32[128,768]{1,0:T(8,128)} %get-tuple-element.109) | copy-start | bytes 1179652
  (57 other events, 92.1 us)

commit v2 on v1

v2 whole, which is shorter than its diff:
```python
import functools

import jax
import jax.numpy as jnp
from jax import lax
from jax.experimental import pallas as pl
from jax.experimental.pallas import tpu as pltpu
from jax.sharding import PartitionSpec as P

HD = 64
EPSILON = 1e-06
MASKED_SCORE = -1e30
MESH = pl.DeviceIdType.MESH
ANY = pl.BlockSpec(memory_space=pl.ANY)
VMEM = pl.BlockSpec(memory_space=pltpu.VMEM)
F32 = jnp.float32
BF16 = jnp.bfloat16


def split_dp(dp):
    inner = 2 ** ((dp.bit_length() - 1) // 2)
    return dp // inner, inner


def place_of(inner):
    d = lax.axis_index("dp")
    return lax.div(d, inner), lax.rem(d, inner), lax.axis_index("tensor")


def across(t):
    return lax.rem(t + 2, 4), t + 1 - 2 * lax.rem(t, 2)


def meet(devices):
    barrier = pltpu.get_barrier_semaphore()
    for device in devices:
        pl.semaphore_signal(barrier, inc=1, device_id=device, device_id_type=MESH)
    pl.semaphore_wait(barrier, len(devices))


def send(source, target, send_sem, recv_sem, device):
    copy = pltpu.make_async_remote_copy(
        src_ref=source,
        dst_ref=target,
        send_sem=send_sem,
        recv_sem=recv_sem,
        device_id=device,
        device_id_type=MESH,
    )
    copy.start()
    return copy


def gather_kernel(dp, own, out, *sems):
    take = Gather(1, dp, out, sems)
    out[0, take.t] = own[...]
    meet(take.friends())
    take.start()
    take.complete(0)
    take.finish()


def gather(own, dp, ident):
    return pl.pallas_call(
        functools.partial(gather_kernel, dp),
        out_shape=jax.ShapeDtypeStruct((1, 4) + own.shape, own.dtype),
        in_specs=[VMEM],
        out_specs=VMEM,
        scratch_shapes=gather_sems(1),
        compiler_params=pltpu.CompilerParams(collective_id=ident, has_side_effects=True),
        name="gather",
    )(own)


def fetch_kernel(outer, inner, count, *refs):
    cut = Cut(refs)
    extra = Fetch(outer, inner, cut(count), cut(count), cut(count), cut(5))
    meet(extra.zdev[1:] + extra.xdev)
    extra.start()
    extra.settle()
    for turn in extra.turns():
        turn()
    extra.finish()


def fetch(owns, outer, inner, ident):
    count = len(owns)
    return pl.pallas_call(
        functools.partial(fetch_kernel, outer, inner, count),
        out_shape=fetch_outs(owns, outer * inner),
        in_specs=[ANY] * count,
        out_specs=[ANY] * count,
        scratch_shapes=fetch_scratch(owns, outer, inner),
        compiler_params=pltpu.CompilerParams(collective_id=ident, has_side_effects=True),
        name="fetch",
    )(*owns)


def push_kernel(outer, inner, count, *refs):
    cut = Cut(refs)
    extra = Push(outer, inner, cut(count), cut(count), cut(3 * count), cut(6))
    meet(extra.zdev[:-1] + extra.xdev)
    extra.start()
    for turn in extra.turns():
        turn()
    extra.finish()


def push(parts, outer, inner, ident):
    count = len(parts)
    return pl.pallas_call(
        functools.partial(push_kernel, outer, inner, count),
        out_shape=push_outs(parts, outer),
        in_specs=[ANY] * count,
        out_specs=[ANY] * count,
        scratch_shapes=push_scratch(parts, outer, inner),
        compiler_params=pltpu.CompilerParams(collective_id=ident, has_side_effects=True),
        name="push",
    )(*parts)


def nearest(index, size, step):
    table = [sorted(range(size), key=lambda other: (abs(other - at), other)) for at in range(size)]
    found = 0
    for at in range(size):
        found = found + jnp.where(index == at, table[at][step], 0)
    return found


class Gather:
    def __init__(self, outer, inner, table, sems):
        self.outer, self.table = outer, table
        self.zs, self.zr, self.ys, self.yr, self.cs, self.cr = sems
        self.dz, self.dx, self.t = place_of(inner)
        self.d = lax.axis_index("dp")
        ty, tc = across(self.t)
        self.ty = ty
        self.pair, self.core = (self.d, ty), (self.d, tc)
        self.source = [nearest(self.dz, outer, step) for step in range(outer)]
        self.zdev = [(source * inner + self.dx, self.t) for source in self.source]
        self.zc, self.yc, self.cc, self.dc = [None], [], [], []

    def friends(self):
        return self.zdev[1:] + [self.pair, self.core]

    def start(self):
        own = self.table.at[self.dz, self.t]
        for step in range(1, self.outer):
            away = lax.rem(self.source[step] - self.dz + self.outer, self.outer)
            self.zc.append(send(own, own, self.zs.at[away], self.zr.at[away], self.zdev[step]))
        self.forward(0)

    def arrive(self, step):
        block = self.table.at[self.source[step], self.t]
        away = lax.rem(self.dz - self.source[step] + self.outer, self.outer)
        pltpu.make_async_remote_copy(
            src_ref=block,
            dst_ref=block,
            send_sem=self.zs.at[away],
            recv_sem=self.zr.at[away],
            device_id=self.zdev[step],
            device_id_type=MESH,
        ).wait_recv()
        self.forward(step)

    def forward(self, step):
        source = self.source[step]
        away = lax.rem(source - self.dz + self.outer, self.outer)
        block = self.table.at[source, self.t]
        self.yc.append(send(block, block, self.ys.at[step], self.yr.at[step], self.pair))
        self.cc.append(send(block, block, self.cs.at[step], self.cr.at[step], self.core))

    def complete(self, step):
        self.yc[step].wait_recv()
        at = self.outer + step
        block = self.table.at[self.source[step], self.ty]
        self.dc.append(send(block, block, self.cs.at[at], self.cr.at[at], self.core))
        self.cc[step].wait_recv()
        self.dc[step].wait_recv()

    def finish(self):
        for copy in self.zc[1:] + self.yc + self.cc + self.dc:
            copy.wait_send()


class Scatter:
    def __init__(self, outer, inner, part, room, sems):
        self.outer, self.part = outer, part
        self.from_c, self.sum_c, self.from_y, self.sum_y, self.from_z = room
        self.cs, self.cr, self.ys, self.yr, self.zs, self.zr = sems
        dz, dx, t = place_of(inner)
        d = lax.axis_index("dp")
        ty, tc = across(t)
        self.dz, self.y, self.c = dz, lax.div(t, 2), lax.rem(t, 2)
        self.pair, self.core = (d, ty), (d, tc)
        self.source = [nearest(dz, outer, step) for step in range(outer)]
        self.zdev = [(source * inner + dx, t) for source in self.source]
        self.cc, self.yc, self.zc = {}, {}, {}

    def core_send(self, step):
        self.cc[step] = send(
            self.part.at[self.source[step], :, 1 - self.c],
            self.from_c.at[step],
            self.cs.at[step],
            self.cr.at[step],
            self.core,
        )

    def pair_send(self, step):
        self.cc[step].wait_recv()
        mine = self.part[self.source[step], :, self.c].astype(F32)
        self.sum_c[step] = (mine + self.from_c[step].astype(F32)).astype(BF16)
        self.yc[step] = send(
            self.sum_c.at[step, 1 - self.y],
            self.from_y.at[step],
            self.ys.at[step],
            self.yr.at[step],
            self.pair,
        )

    def outer_send(self, step):
        self.yc[step].wait_recv()
        total = self.sum_c[step, self.y].astype(F32) + self.from_y[step].astype(F32)
        if step == 0:
            return total
        self.sum_y[step - 1] = total.astype(BF16)
        away = lax.rem(self.source[step] - self.dz + self.outer, self.outer)
        self.zc[step] = send(
            self.sum_y.at[step - 1],
            self.from_z.at[away - 1],
            self.zs.at[away - 1],
            self.zr.at[away - 1],
            self.zdev[step],
        )
        return None

    def total(self, total):
        for step in range(1, self.outer):
            away = lax.rem(self.dz - self.source[step] + self.outer, self.outer)
            block = self.from_z.at[away - 1]
            pltpu.make_async_remote_copy(
                src_ref=block,
                dst_ref=block,
                send_sem=self.zs.at[away - 1],
                recv_sem=self.zr.at[away - 1],
                device_id=self.zdev[step],
                device_id_type=MESH,
            ).wait_recv()
            total = total + self.from_z[away - 1].astype(F32)
        return total

    def finish(self):
        for group in (self.cc, self.yc, self.zc):
            for step in group:
                group[step].wait_send()


def gather_sems(outer):
    dma = pltpu.SemaphoreType.DMA
    return [dma((outer,)) for _ in range(4)] + [dma((2 * outer,)) for _ in range(2)]


def scatter_sems(outer):
    dma = pltpu.SemaphoreType.DMA
    return [dma((outer,)) for _ in range(6)]


def scatter_room(outer, rows, width):
    low = max(outer - 1, 1)
    return [
        pltpu.VMEM((outer, 2, rows, width), BF16),
        pltpu.VMEM((outer, 2, rows, width), BF16),
        pltpu.VMEM((outer, rows, width), BF16),
        pltpu.VMEM((low, rows, width), BF16),
        pltpu.VMEM((low, rows, width), BF16),
    ]


def pipeline(outer, take, give, compute, fill):
    fill = iter(fill)

    def filler(count):
        for _ in range(count):
            work = next(fill, None)
            if work is not None:
                work()

    take.start()
    filler(1)
    take.arrive(1)
    take.complete(0)
    compute(0)
    give.core_send(0)
    give.pair_send(0)
    for step in range(1, outer):
        if step == 1:
            take.complete(1)
        if step + 1 < outer:
            take.arrive(step + 1)
        if step > 1:
            give.pair_send(step - 1)
            take.complete(step)
        compute(step)
        give.core_send(step)
        if step == 1:
            filler(1)
        if step > 2:
            give.outer_send(step - 2)
    filler(1)
    give.pair_send(outer - 1)
    filler(2)
    if outer > 2:
        give.outer_send(outer - 2)
    filler(2)
    give.outer_send(outer - 1)
    filler(100)
    return give.outer_send(0)


class Fetch:
    def __init__(self, outer, inner, owns, outs, holds, sems):
        self.outer, self.inner, self.owns, self.outs, self.holds = outer, inner, owns, outs, holds
        self.zs, self.zr, self.xs, self.xr, self.ls = sems
        self.dz, dx, t = place_of(inner)
        self.dx, self.d = dx, lax.axis_index("dp")
        self.source = [nearest(self.dz, outer, step) for step in range(outer)]
        self.zdev = [(source * inner + dx, t) for source in self.source]
        self.xdev = [(self.dz * inner + lax.rem(dx + j, inner), t) for j in range(1, inner)]
        self.zc, self.xc, self.into, self.back = [], [], [], []

    def own(self, i, where):
        return self.owns[i].at[where if self.owns[i].shape[0] == self.outer else 0]

    def copy(self, i, step):
        away = lax.rem(self.source[step] - self.dz + self.outer, self.outer)
        at = i * self.outer + away
        return pltpu.make_async_remote_copy(
            src_ref=self.own(i, self.source[step]),
            dst_ref=self.outs[i].at[self.d],
            send_sem=self.zs.at[at],
            recv_sem=self.zr.at[at],
            device_id=self.zdev[step],
            device_id_type=MESH,
        )

    def start(self):
        for i in range(len(self.owns)):
            here = self.own(i, self.dz)
            self.into.append(pltpu.make_async_copy(here, self.holds[i], self.ls.at[i]))
            self.into[i].start()
            for step in range(1, self.outer):
                self.zc.append(self.copy(i, step))
                self.zc[-1].start()
            self.spread(i, 0, here, self.outs[i].at[self.d])

    def spread(self, i, step, block, target):
        for j in range(1, self.inner):
            at = (i * self.outer + step) * self.inner + j
            self.xc.append(
                send(block, target, self.xs.at[at], self.xr.at[at], self.xdev[j - 1])
            )

    def settle(self):
        for i, into in enumerate(self.into):
            into.wait()
            self.back.append(
                pltpu.make_async_copy(self.holds[i], self.outs[i].at[self.d], self.ls.at[i])
            )
            self.back[i].start()

    def turn(self, i, step):
        source = self.source[step]
        block = self.outs[i].at[source * self.inner + self.dx]
        away = lax.rem(self.dz - source + self.outer, self.outer)
        at = i * self.outer + away
        pltpu.make_async_remote_copy(
            src_ref=block,
            dst_ref=block,
            send_sem=self.zs.at[at],
            recv_sem=self.zr.at[at],
            device_id=self.zdev[step],
            device_id_type=MESH,
        ).wait_recv()
        self.spread(i, step, block, block)

    def turns(self):
        return [
            functools.partial(self.turn, i, step)
            for i in range(len(self.owns))
            for step in range(1, self.outer)
        ]

    def finish(self):
        for copy in self.xc:
            copy.wait_recv()
        for copy in self.xc + self.zc:
            copy.wait_send()
        for copy in self.back:
            copy.wait()


def fetch_outs(owns, dp):
    return [jax.ShapeDtypeStruct((dp,) + own.shape[1:], own.dtype) for own in owns]


def fetch_scratch(owns, outer, inner):
    dma = pltpu.SemaphoreType.DMA
    count = max(len(owns), 1)
    return [pltpu.VMEM(own.shape[1:], own.dtype) for own in owns] + [
        dma((count * outer,)),
        dma((count * outer,)),
        dma((count * outer * inner,)),
        dma((count * outer * inner,)),
        dma((count,)),
    ]


class Push:
    def __init__(self, outer, inner, parts, outs, room, sems):
        count = len(parts)
        self.outer, self.inner, self.parts, self.outs = outer, inner, parts, outs
        self.froms, self.mine, self.sums = room[:count], room[count : 2 * count], room[2 * count :]
        self.xs, self.xr, self.zs, self.zr, self.ls, self.ks = sems
        self.dz, dx, t = place_of(inner)
        self.dx = dx
        near = [nearest(self.dz, outer, step) for step in range(outer)]
        self.source = near[:0:-1] + near[:1]
        self.zdev = [(source * inner + dx, t) for source in self.source]
        self.xdev = [(self.dz * inner + lax.rem(dx + j, inner), t) for j in range(1, inner)]
        self.xc, self.zc, self.loads, self.keeps = {}, [], {}, []

    def start(self):
        for i in range(len(self.parts)):
            for step, source in enumerate(self.source):
                for j in range(1, self.inner):
                    slot = source * self.inner + lax.rem(self.dx + j, self.inner)
                    at = (i * self.outer + step) * self.inner + j
                    self.xc[i, step, j] = send(
                        self.parts[i].at[slot],
                        self.froms[i].at[j - 1, step],
                        self.xs.at[at],
                        self.xr.at[at],
                        self.xdev[j - 1],
                    )
                self.loads[i, step] = pltpu.make_async_copy(
                    self.parts[i].at[source * self.inner + self.dx],
                    self.mine[i].at[step],
                    self.ls.at[i * self.outer + step],
                )
                self.loads[i, step].start()

    def turn(self, i, step):
        self.loads[i, step].wait()
        total = self.mine[i][step].astype(F32)
        for j in range(1, self.inner):
            self.xc[i, step, j].wait_recv()
            total = total + self.froms[i][j - 1, step].astype(F32)
        self.sums[i][step] = total.astype(self.sums[i].dtype)
        target = self.outs[i].at[self.dz]
        if step < self.outer - 1:
            away = lax.rem(self.source[step] - self.dz + self.outer, self.outer)
            at = i * self.outer + away
            self.zc.append(
                send(self.sums[i].at[step], target, self.zs.at[at], self.zr.at[at], self.zdev[step])
            )
        else:
            self.keeps.append(
                pltpu.make_async_copy(self.sums[i].at[step], target, self.ks.at[i])
            )
            self.keeps[-1].start()

    def turns(self):
        return [
            functools.partial(self.turn, i, step)
            for i in range(len(self.parts))
            for step in range(self.outer)
        ]

    def finish(self):
        for copy in self.zc:
            copy.wait_recv()
            copy.wait_send()
        for key in self.xc:
            self.xc[key].wait_send()
        for copy in self.keeps:
            copy.wait()


def push_outs(parts, outer):
    return [jax.ShapeDtypeStruct((outer,) + part.shape[1:], part.dtype) for part in parts]


def push_scratch(parts, outer, inner):
    dma = pltpu.SemaphoreType.DMA
    count = max(len(parts), 1)
    across_x = [pltpu.VMEM((inner - 1, outer) + part.shape[1:], part.dtype) for part in parts]
    own = [pltpu.VMEM((outer,) + part.shape[1:], part.dtype) for part in parts]
    return (
        across_x
        + own
        + own
        + [
            dma((count * outer * inner,)),
            dma((count * outer * inner,)),
            dma((count * outer,)),
            dma((count * outer,)),
            dma((count * outer,)),
            dma((count,)),
        ]
    )


class Cut:
    def __init__(self, refs):
        self.refs, self.at = refs, 0

    def __call__(self, count):
        self.at += count
        return self.refs[self.at - count : self.at]


def ffn_forward_kernel(outer, inner, kinds, count, *refs):
    cut = Cut(refs)
    resid, gain, mix, w_in_any, w_down_any = cut(5)
    owns = cut(count)
    out, b_out, gu_out = cut(3)
    fetched = cut(count)
    w_in, w_down, b, gu, part = cut(5)
    room, take_sems, give_sems = cut(5), cut(6), cut(6)
    load_sem, keep_b, keep_gu = cut(3)
    extra = Fetch(outer, inner, owns, fetched, cut(count), cut(5)) if count else None
    rows, width = resid.shape
    third = w_down.shape[1]
    slim = third // kinds
    loads = [
        pltpu.make_async_copy(w_in_any, w_in, load_sem.at[0]),
        pltpu.make_async_copy(w_down_any, w_down, load_sem.at[1]),
    ]
    for load in loads:
        load.start()
    take = Gather(outer, inner, b, take_sems)
    give = Scatter(outer, inner, part, room, give_sems)
    x = resid[...]
    inverse = lax.rsqrt(jnp.mean(x * x, axis=-1, keepdims=True) + EPSILON)
    b[take.dz, take.t] = (x * inverse * gain[...]).astype(BF16)
    meet(take.friends() + (extra.xdev if count else []))
    keeps = []

    def compute(step):
        source = take.source[step]
        if step == 0:
            for load in loads:
                load.wait()

        @pl.loop(0, 2)
        def _(half):
            rows_in = b[source, pl.ds(2 * half, 2)].reshape(2 * rows, width)
            both = dot(rows_in, w_in[...])
            gu[source, half] = both.astype(BF16)
            gate, up = both[:, :third], both[:, third:]
            hidden = gate * jax.nn.sigmoid(gate) * up
            pieces = []
            for e in range(kinds):
                piece = hidden[:, e * slim : (e + 1) * slim]
                if e < kinds - 1:
                    piece = piece * mix[source, half, :, e : e + 1]
                pieces.append(piece.astype(BF16))
            hidden = jnp.concatenate(pieces, axis=1)
            sent = dot_nt(hidden, w_down[...])
            part[source, half] = sent.astype(BF16).reshape(2, rows, width)

        keeps.append(pltpu.make_async_copy(b.at[source], b_out.at[source], keep_b.at[step]))
        keeps.append(pltpu.make_async_copy(gu.at[source], gu_out.at[source], keep_gu.at[step]))
        keeps[-1].start()
        keeps[-2].start()

    fill = []
    if count:
        turns = extra.turns()

        def begin():
            extra.start()
            extra.settle()

        def rest():
            for turn in turns:
                turn()

        fill = [begin, rest]
    total = pipeline(outer, take, give, compute, fill)
    out[...] = resid[...] + give.total(total)
    take.finish()
    give.finish()
    if count:
        extra.finish()
    for keep in keeps:
        keep.wait()


def ffn_forward(resid, gain, mix, w_in, w_down, owns, outer, inner, ident):
    dma = pltpu.SemaphoreType.DMA
    rows, width = resid.shape
    third = w_down.shape[1]
    kinds = mix.shape[-1] + 1
    count = len(owns)
    return pl.pallas_call(
        functools.partial(ffn_forward_kernel, outer, inner, kinds, count),
        out_shape=[
            jax.ShapeDtypeStruct((rows, width), F32),
            jax.ShapeDtypeStruct((outer, 4, rows, width), BF16),
            jax.ShapeDtypeStruct((outer, 2, 2 * rows, 2 * third), BF16),
        ]
        + fetch_outs(owns, outer * inner),
        in_specs=[VMEM, VMEM, VMEM, ANY, ANY] + [ANY] * count,
        out_specs=[VMEM, ANY, ANY] + [ANY] * count,
        scratch_shapes=[
            pltpu.VMEM(w_in.shape, BF16),
            pltpu.VMEM(w_down.shape, BF16),
            pltpu.VMEM((outer, 4, rows, width), BF16),
            pltpu.VMEM((outer, 2, 2 * rows, 2 * third), BF16),
            pltpu.VMEM((outer, 2, 2, rows, width), BF16),
        ]
        + scatter_room(outer, rows, width)
        + gather_sems(outer)
        + scatter_sems(outer)
        + [dma((2,)), dma((outer,)), dma((outer,))]
        + (fetch_scratch(owns, outer, inner) if count else []),
        compiler_params=pltpu.CompilerParams(
            collective_id=ident, has_side_effects=True, vmem_limit_bytes=62 << 20
        ),
        name="ffn_forward",
    )(resid, gain, mix, w_in, w_down, *owns)


def ffn_backward_kernel(outer, inner, kinds, count, *refs):
    cut = Cut(refs)
    grad_y, resid, gain, mix, w_in_any, w_down_any, b_any, gu_any = cut(8)
    parts = cut(count)
    out, gain_out, grad_in, grad_down = cut(4)
    pushed = cut(count)
    w_in, w_down, b, gb, gu, dgu, hid, flip, part = cut(9)
    room, take_sems, give_sems = cut(5), cut(6), cut(6)
    load_sem, load_gu = cut(2)
    extra = Push(outer, inner, parts, pushed, cut(3 * count), cut(6)) if count else None
    rows, width = resid.shape
    tall = outer * 4 * rows
    third = w_down.shape[1]
    slim = third // kinds
    loads = [
        pltpu.make_async_copy(source, target, load_sem.at[i])
        for i, (source, target) in enumerate(
            ((b_any, b), (w_down_any, w_down), (w_in_any, w_in))
        )
    ]
    for load in loads:
        load.start()
    take = Gather(outer, inner, gb, take_sems)
    give = Scatter(outer, inner, part, room, give_sems)
    fills = [
        pltpu.make_async_copy(gu_any.at[source], gu.at[source], load_gu.at[step])
        for step, source in enumerate(take.source)
    ]
    for fill in fills:
        fill.start()
    gb[take.dz, take.t] = grad_y[...].astype(BF16)
    meet(take.friends() + (extra.xdev if count else []))

    def compute(step):
        source = take.source[step]
        if step == 0:
            loads[1].wait()
            loads[2].wait()
        fills[step].wait()

        @pl.loop(0, 2)
        def _(half):
            rows_in = gb[source, pl.ds(2 * half, 2)].reshape(2 * rows, width)
            grad_hidden = dot(rows_in, w_down[...])
            both = gu[source, half].astype(F32)
            gate, up = both[:, :third], both[:, third:]
            sigma = jax.nn.sigmoid(gate)
            act = gate * sigma
            slope = sigma * (1.0 + gate * (1.0 - sigma))
            hidden, grad_gate, grad_up = act * up, grad_hidden * up * slope, grad_hidden * act
            for e in range(kinds):
                here = slice(e * slim, (e + 1) * slim)
                there = slice(third + e * slim, third + (e + 1) * slim)
                scale = mix[source, half, :, e : e + 1] if e < kinds - 1 else 1.0
                hid[source, half, :, here] = (hidden[:, here] * scale).astype(BF16)
                dgu[source, half, :, here] = (grad_gate[:, here] * scale).astype(BF16)
                dgu[source, half, :, there] = (grad_up[:, here] * scale).astype(BF16)
            sent = dot_nt(dgu[source, half], w_in[...])
            part[source, half] = sent.astype(BF16).reshape(2, rows, width)

    def turned(table):
        @pl.loop(0, outer * 4)
        def _(at):
            block = table[lax.div(at, 4), lax.rem(at, 4)]
            flip[:, pl.ds(pl.multiple_of(at * rows, rows), rows)] = jnp.transpose(block)

    def weigh(target, source, low, high):
        values = source[...].reshape(tall, source.shape[-1])

        @pl.loop(0, width // 256)
        def _(at):
            here = pl.ds(pl.multiple_of(at * 256, 256), 256)
            target[here, low:high] = dot(flip[here, :], values[:, low:high]).astype(BF16)

    def begin():
        if count:
            extra.start()
        loads[0].wait()
        turned(b)

    def between():
        if count:
            for turn in extra.turns():
                turn()

    def pieces(total):
        return [(low, min(low + 256, total)) for low in range(0, total, 256)]

    fill = [begin, between]
    fill += [functools.partial(weigh, grad_in, dgu, *span) for span in pieces(2 * third)]
    fill += [functools.partial(turned, gb)]
    fill += [functools.partial(weigh, grad_down, hid, *span) for span in pieces(third)]
    total = pipeline(outer, take, give, compute, fill)
    grad_b = give.total(total)
    x = resid[...]
    inverse = lax.rsqrt(jnp.mean(x * x, axis=-1, keepdims=True) + EPSILON)
    unit = x * inverse
    gain_out[...] = jnp.sum(grad_b * unit, axis=0, keepdims=True)
    out[...] = grad_y[...] + norm_back(grad_b, gain[...], unit, inverse)
    take.finish()
    give.finish()
    if count:
        extra.finish()


def ffn_backward(grad_y, resid, gain, mix, w_in, w_down, b, both, parts, outer, inner, ident):
    dma = pltpu.SemaphoreType.DMA
    rows, width = resid.shape
    third = w_down.shape[1]
    kinds = mix.shape[-1] + 1
    count = len(parts)
    return pl.pallas_call(
        functools.partial(ffn_backward_kernel, outer, inner, kinds, count),
        out_shape=[
            jax.ShapeDtypeStruct((rows, width), F32),
            jax.ShapeDtypeStruct((1, width), F32),
            jax.ShapeDtypeStruct((width, 2 * third), BF16),
            jax.ShapeDtypeStruct((width, third), BF16),
        ]
        + push_outs(parts, outer),
        in_specs=[VMEM, VMEM, VMEM, VMEM, ANY, ANY, ANY, ANY] + [ANY] * count,
        out_specs=[VMEM, VMEM, VMEM, VMEM] + [ANY] * count,
        scratch_shapes=[
            pltpu.VMEM(w_in.shape, BF16),
            pltpu.VMEM(w_down.shape, BF16),
            pltpu.VMEM((outer, 4, rows, width), BF16),
            pltpu.VMEM((outer, 4, rows, width), BF16),
            pltpu.VMEM((outer, 2, 2 * rows, 2 * third), BF16),
            pltpu.VMEM((outer, 2, 2 * rows, 2 * third), BF16),
            pltpu.VMEM((outer, 2, 2 * rows, third), BF16),
            pltpu.VMEM((width, outer * 4 * rows), BF16),
            pltpu.VMEM((outer, 2, 2, rows, width), BF16),
        ]
        + scatter_room(outer, rows, width)
        + gather_sems(outer)
        + scatter_sems(outer)
        + [dma((3,)), dma((outer,))]
        + (push_scratch(parts, outer, inner) if count else []),
        compiler_params=pltpu.CompilerParams(
            collective_id=ident, has_side_effects=True, vmem_limit_bytes=63 << 20
        ),
        name="ffn_backward",
    )(grad_y, resid, gain, mix, w_in, w_down, b, both, *parts)


def swap_halves(values):
    width = values.shape[1]
    lane = lax.broadcasted_iota(jnp.int32, values.shape, 1)
    low = lax.rem(lane, HD) < HD // 2
    return jnp.where(
        low, pltpu.roll(values, width - HD // 2, 1), pltpu.roll(values, HD // 2, 1)
    )


def allowed_rows(marks, spot, top):
    del top
    return (spot >= marks[:, 1:2]) & (spot <= marks[:, 0:1])


def attn_forward_kernel(outer, inner, count, *refs):
    dp = outer * inner
    cut = Cut(refs)
    x_in, gain, weight, tables, marks, spot = cut(6)
    owns = cut(count)
    out, a_out, qk_out, v_out, lse_out, att_out = cut(6)
    fetched = cut(count)
    w, a, qk, v, att, part = cut(6)
    room, take_sems, give_sems = cut(5), cut(6), cut(6)
    load_sem, keep_sem = cut(2)
    extra = Fetch(outer, inner, owns, fetched, cut(count), cut(5))
    turns = extra.turns()
    rows, width = x_in.shape
    heads_width = w.shape[1] // 4
    heads = heads_width // HD
    load = pltpu.make_async_copy(weight, w, load_sem)
    load.start()
    take = Gather(1, dp, a, take_sems)
    give = Scatter(1, dp, part, room, give_sems)
    x = x_in[...]
    inverse = lax.rsqrt(jnp.mean(x * x, axis=-1, keepdims=True) + EPSILON)
    a[0, take.t] = (x * inverse * gain[...]).astype(BF16)
    meet(take.friends() + extra.zdev[1:] + extra.xdev)
    take.start()
    extra.start()
    load.wait()

    def project(block):
        both = dot(a[0, block], w[:, : 3 * heads_width])
        raw = both[:, : 2 * heads_width]
        times = 2 * heads_width // tables.shape[-1]
        cosine = jnp.concatenate([tables[0, block]] * times, axis=1)
        sine = jnp.concatenate([tables[1, block]] * times, axis=1)
        qk[block] = (raw * cosine + swap_halves(raw) * sine).astype(BF16)
        v[block] = both[:, 2 * heads_width :].astype(BF16)

    project(take.t)
    take.complete(0)
    for other in range(1, 4):
        project(lax.rem(take.t + other, 4))
    keeps = [pltpu.make_async_copy(a.at[0], a_out, keep_sem.at[0])]
    keeps.append(pltpu.make_async_copy(qk, qk_out, keep_sem.at[1]))
    keeps.append(pltpu.make_async_copy(v, v_out, keep_sem.at[2]))
    for keep in keeps:
        keep.start()

    def attend(block):
        keys = qk[...].reshape(4 * rows, 2 * heads_width)
        values = v[...].reshape(4 * rows, heads_width)
        allowed = allowed_rows(marks[block], spot[...], 0)
        pieces = []
        for head in range(heads):
            here = slice(head * HD, (head + 1) * HD)
            there = slice(heads_width + head * HD, heads_width + (head + 1) * HD)
            scores = dot_nt(qk[block, :, here], keys[:, there])
            scores = jnp.where(allowed, scores * HD ** (-0.5), MASKED_SCORE)
            top = jnp.max(scores, axis=-1, keepdims=True)
            expo = jnp.exp(scores - top)
            total = jnp.sum(expo, axis=-1, keepdims=True)
            probs = (expo / total).astype(BF16)
            lse_out[block, :, head : head + 1] = top + jnp.log(total)
            pieces.append(dot(probs, values[:, here]).astype(BF16))
        att[block] = jnp.concatenate(pieces, axis=1)
        sent = dot_nt(att[block], w[:, 3 * heads_width :]).astype(BF16)
        part[0, lax.div(block, 2), lax.rem(block, 2)] = sent

    y, c = give.y, give.c
    extra.settle()
    attend(2 * (1 - y) + 1 - c)
    attend(2 * y + 1 - c)
    give.core_send(0)
    turns[0]()
    attend(2 * (1 - y) + c)
    attend(2 * y + c)
    give.pair_send(0)
    for turn in turns[1:]:
        turn()
    keeps.append(pltpu.make_async_copy(att, att_out, keep_sem.at[3]))
    keeps[-1].start()
    out[...] = x_in[...] + give.outer_send(0)
    take.finish()
    give.finish()
    extra.finish()
    for keep in keeps:
        keep.wait()


def attn_forward(x, gain, weight, tables, marks, spot, owns, outer, inner, ident):
    count = len(owns)
    dma = pltpu.SemaphoreType.DMA
    rows, width = x.shape
    slim = weight.shape[1] // 4
    kept = [(4, rows, width), (4, rows, 2 * slim), (4, rows, slim)]
    return pl.pallas_call(
        functools.partial(attn_forward_kernel, outer, inner, count),
        out_shape=[jax.ShapeDtypeStruct((rows, width), F32)]
        + [jax.ShapeDtypeStruct(shape, BF16) for shape in kept]
        + [
            jax.ShapeDtypeStruct((4, rows, 8), F32),
            jax.ShapeDtypeStruct((4, rows, slim), BF16),
        ]
        + fetch_outs(owns, outer * inner),
        in_specs=[VMEM, VMEM, ANY, VMEM, VMEM, VMEM] + [ANY] * count,
        out_specs=[VMEM, ANY, ANY, ANY, VMEM, ANY] + [ANY] * count,
        scratch_shapes=[
            pltpu.VMEM(weight.shape, BF16),
            pltpu.VMEM((1, 4, rows, width), BF16),
            pltpu.VMEM(kept[1], BF16),
            pltpu.VMEM(kept[2], BF16),
            pltpu.VMEM(kept[2], BF16),
            pltpu.VMEM((1, 2, 2, rows, width), BF16),
        ]
        + scatter_room(1, rows, width)
        + gather_sems(1)
        + scatter_sems(1)
        + [dma, dma((4,))]
        + fetch_scratch(owns, outer, inner),
        compiler_params=pltpu.CompilerParams(collective_id=ident, has_side_effects=True),
        name="attn_forward",
    )(x, gain, weight, tables, marks, spot, *owns)


def attn_backward_kernel(outer, inner, count, *refs):
    dp = outer * inner
    cut = Cut(refs)
    grad_in, x_in, gain, weight, tables, marks, spot = cut(7)
    a_in, qk_in, v_in, lse, att_in = cut(5)
    parts = cut(count)
    out, gain_out, grad_w = cut(3)
    pushed = cut(count)
    w, a, qk, v, att, ga, g_att, raw, part = cut(9)
    room, take_sems, give_sems = cut(5), cut(6), cut(6)
    (load_sem,) = cut(1)
    extra = Push(outer, inner, parts, pushed, cut(3 * count), cut(6))
    turns = extra.turns()
    rows, width = x_in.shape
    tall = 4 * rows
    heads_width = w.shape[1] // 4
    heads = heads_width // HD
    loads = [
        pltpu.make_async_copy(source, target, load_sem.at[i])
        for i, (source, target) in enumerate(
            ((weight, w), (qk_in, qk), (v_in, v), (att_in, att), (a_in, a))
        )
    ]
    for load in loads:
        load.start()
    take = Gather(1, dp, ga, take_sems)
    give = Scatter(1, dp, part, room, give_sems)
    ga[0, take.t] = grad_in[...].astype(BF16)
    meet(take.friends() + extra.zdev[:-1] + extra.xdev)
    take.start()
    extra.start()
    for load in loads:
        load.wait()
    take.complete(0)
    turns[0]()
    grads = ga[...].reshape(tall, width)
    g_att[...] = dot(grads, w[:, 3 * heads_width :]).astype(BF16)
    all_qk = qk[...].reshape(tall, 2 * heads_width)
    all_v = v[...].reshape(tall, heads_width)
    all_marks = marks[...].reshape(tall, marks.shape[-1])
    all_lse = lse[...].reshape(tall, lse.shape[-1])
    allowed = allowed_rows(all_marks, spot[...], 0)
    q_grads, k_grads, v_grads = [], [], []
    for head in range(heads):
        here = slice(head * HD, (head + 1) * HD)
        there = slice(heads_width + head * HD, heads_width + (head + 1) * HD)
        query, key = all_qk[:, here], all_qk[:, there]
        scores = dot_nt(query, key)
        scores = jnp.where(allowed, scores * HD ** (-0.5), MASKED_SCORE)
        probs = jnp.exp(scores - all_lse[:, head : head + 1])
        grad_probs = dot_nt(g_att[:, here], all_v[:, here])
        inner = jnp.sum(grad_probs * probs, axis=-1, keepdims=True)
        grad_scores = (probs * (grad_probs - inner)).astype(BF16)
        v_grads.append(dot_tn(probs.astype(BF16), g_att[:, here]).astype(BF16))
        q_grads.append(dot(grad_scores, key))
        k_grads.append(dot_tn(grad_scores, query))
    rotated = jnp.concatenate(q_grads + k_grads, axis=1) * HD ** (-0.5)
    times = 2 * heads_width // tables.shape[-1]
    cosine = jnp.concatenate([tables[0].reshape(tall, -1)] * times, axis=1)
    sine = jnp.concatenate([tables[1].reshape(tall, -1)] * times, axis=1)
    raw[:, : 2 * heads_width] = (rotated * cosine - swap_halves(rotated) * sine).astype(BF16)
    raw[:, 2 * heads_width :] = jnp.concatenate(v_grads, axis=1)
    def back(block):
        at = pl.ds(pl.multiple_of(block * rows, rows), rows)
        sent = dot_nt(raw[at, :], w[:, : 3 * heads_width]).astype(BF16)
        part[0, lax.div(block, 2), lax.rem(block, 2)] = sent

    turns[1]()
    y, c = give.y, give.c
    back(2 * (1 - y) + 1 - c)
    back(2 * y + 1 - c)
    give.core_send(0)
    back(2 * (1 - y) + c)
    back(2 * y + c)
    give.pair_send(0)
    turns[2]()
    grad_w[:, : 3 * heads_width] = dot_tn(a[...].reshape(tall, width), raw[...]).astype(BF16)
    grad_w[:, 3 * heads_width :] = dot_tn(grads, att[...].reshape(tall, heads_width)).astype(
        BF16
    )
    grad_a = give.outer_send(0)
    x = x_in[...]
    inverse = lax.rsqrt(jnp.mean(x * x, axis=-1, keepdims=True) + EPSILON)
    unit = x * inverse
    gain_out[...] = jnp.sum(grad_a * unit, axis=0, keepdims=True)
    out[...] = grad_in[...] + norm_back(grad_a, gain[...], unit, inverse)
    for turn in turns[3:]:
        turn()
    take.finish()
    give.finish()
    extra.finish()


def attn_backward(grad, x, gain, weight, tables, marks, spot, kept, parts, outer, inner, ident):
    count = len(parts)
    dma = pltpu.SemaphoreType.DMA
    rows, width = x.shape
    slim = weight.shape[1] // 4
    return pl.pallas_call(
        functools.partial(attn_backward_kernel, outer, inner, count),
        out_shape=[
            jax.ShapeDtypeStruct((rows, width), F32),
            jax.ShapeDtypeStruct((1, width), F32),
            jax.ShapeDtypeStruct(weight.shape, BF16),
        ]
        + push_outs(parts, outer),
        in_specs=[VMEM, VMEM, VMEM, ANY, VMEM, VMEM, VMEM, ANY, ANY, ANY, VMEM, ANY]
        + [ANY] * count,
        out_specs=[VMEM, VMEM, VMEM] + [ANY] * count,
        scratch_shapes=[
            pltpu.VMEM(weight.shape, BF16),
            pltpu.VMEM((4, rows, width), BF16),
            pltpu.VMEM((4, rows, 2 * slim), BF16),
            pltpu.VMEM((4, rows, slim), BF16),
            pltpu.VMEM((4, rows, slim), BF16),
            pltpu.VMEM((1, 4, rows, width), BF16),
            pltpu.VMEM((4 * rows, slim), BF16),
            pltpu.VMEM((4 * rows, 3 * slim), BF16),
            pltpu.VMEM((1, 2, 2, rows, width), BF16),
        ]
        + scatter_room(1, rows, width)
        + gather_sems(1)
        + scatter_sems(1)
        + [dma((5,))]
        + push_scratch(parts, outer, inner),
        compiler_params=pltpu.CompilerParams(
            collective_id=ident, has_side_effects=True, vmem_limit_bytes=62 << 20
        ),
        name="attn_backward",
    )(grad, x, gain, weight, tables, marks, spot, *kept, *parts)


def layout(place_row, length_row):
    ends = jnp.cumsum(length_row, dtype=jnp.int32)
    after = place_row[:, None] >= ends[None, :]
    begins = jnp.sum(jnp.where(after, length_row[None, :], 0), axis=1, dtype=jnp.int32)
    return place_row - begins


def rope_tables(position):
    half_width = HD // 2
    freqs = 10000.0 ** (-jnp.arange(half_width, dtype=F32) / half_width)
    angles = position.astype(F32)[:, None] * freqs[None, :]
    cosine, sine = jnp.cos(angles), jnp.sin(angles)
    return jnp.stack(
        [
            jnp.concatenate([cosine] * 4, axis=1),
            jnp.concatenate([-sine, sine, -sine, sine], axis=1),
        ]
    )


def norm_back(grad_normed, gain_row, unit_rows, inverse):
    scaled = grad_normed * gain_row
    return inverse * (scaled - unit_rows * jnp.mean(scaled * unit_rows, axis=-1, keepdims=True))


def dot(left, right):
    return jnp.dot(left, right, preferred_element_type=F32)


def dot_nt(left, right):
    return lax.dot_general(left, right, (((1,), (1,)), ((), ())), preferred_element_type=F32)


def dot_tn(left, right):
    return lax.dot_general(left, right, (((0,), (0,)), ((), ())), preferred_element_type=F32)


def make_body(dp):
    outer, inner = split_dp(dp)

    def body(
        tokens,
        place,
        lengths,
        expert_ids,
        gate_values,
        cotangent,
        gain_attn,
        w_query,
        w_key,
        w_value,
        w_out,
        gain_ffn,
        exp_gate,
        exp_up,
        exp_down,
        dense_gate,
        dense_up,
        dense_down,
    ):
        layers, experts, rows, full = exp_gate.shape
        width = tokens.shape[1]
        slim = full // outer
        count = place.shape[1]
        position = layout(place[0], lengths[0])
        place_row = place[0].astype(F32)
        marks = jnp.stack([place_row, place_row - position.astype(F32)] * 4, axis=1)
        marks = marks.reshape(4, count // 4, 8)
        spot = place_row[None]
        tables = rope_tables(position).reshape(2, 4, count // 4, 128)

        slots = expert_ids[:, None] == jnp.arange(experts, dtype=jnp.int32)[None, :, None, None]
        mix_own = jnp.sum(jnp.where(slots, gate_values[:, None], 0.0), axis=-1)
        gains_own = jnp.pad(
            jnp.concatenate([gain_attn, gain_ffn], axis=0).astype(BF16).astype(F32),
            ((0, 8 - 2 * layers), (0, count - rows)),
        )
        small_own = jnp.concatenate([mix_own.reshape(-1, count), gains_own], axis=0)

        attn_own, ffn_own = [], []
        for level in range(layers):
            attn_own.append(
                jnp.concatenate(
                    [w_query[level], w_key[level], w_value[level], jnp.transpose(w_out[level])],
                    axis=1,
                ).astype(BF16)[None]
            )
            mats = (
                [exp_gate[level, e] for e in range(experts)]
                + [dense_gate[level]]
                + [exp_up[level, e] for e in range(experts)]
                + [dense_up[level]]
                + [jnp.transpose(exp_down[level, e]) for e in range(experts)]
                + [jnp.transpose(dense_down[level])]
            )
            mats = [m.astype(BF16) for m in mats]
            kinds = experts + 1
            ffn_own.append(
                [
                    jnp.stack(
                        [
                            jnp.concatenate(
                                [m[:, k * slim : (k + 1) * slim] for m in group], axis=1
                            )
                            for k in range(outer)
                        ]
                    )
                    for group in (mats[: 2 * kinds], mats[2 * kinds :])
                ]
            )
        small_all, first = fetch([small_own[None], attn_own[0]], outer, inner, 4)
        w_attn = [first.reshape(width, -1)]
        w_ffn = []

        gains = jnp.transpose(small_all[:, layers * experts :, :rows], (1, 0, 2)).reshape(8, width)
        dx = lax.rem(lax.axis_index("dp"), inner)
        mix_all = lax.dynamic_index_in_dim(
            small_all[:, : layers * experts].reshape(outer, inner, layers, experts, count),
            dx,
            axis=1,
            keepdims=False,
        )
        mixing = [
            jnp.transpose(mix_all[:, level], (0, 2, 1)).reshape(outer, 2, count // 2, experts)
            for level in range(layers)
        ]

        state = tokens.astype(F32)
        kept_attn, kept_ffn = [], []
        for level in range(layers):
            before = state
            state, *kept, w_in, w_down = attn_forward(
                before,
                gains[level][None],
                w_attn[level],
                tables,
                marks,
                spot,
                ffn_own[level],
                outer,
                inner,
                0,
            )
            kept_attn.append((before, kept))
            w_ffn.append((w_in.reshape(width, -1), w_down.reshape(width, -1)))
            resid = state
            more = [attn_own[level + 1]] if level + 1 < layers else []
            state, b_in, both, *fetched = ffn_forward(
                resid,
                gains[layers + level][None],
                mixing[level],
                *w_ffn[level],
                more,
                outer,
                inner,
                2 if more else 5,
            )
            w_attn += [block.reshape(width, -1) for block in fetched]
            kept_ffn.append((resid, b_in, both))
        mixed = state.astype(BF16)

        grad = cotangent.astype(F32)
        part_gains = [None] * (2 * layers)
        pushed_ffn, pushed_attn = [None] * layers, [None] * layers
        grad_attn = None
        for level in reversed(range(layers)):
            resid, b_in, both = kept_ffn[level]
            more = [] if grad_attn is None else [grad_attn.reshape(dp, rows, -1)]
            grad, part_gain, grad_in, grad_down, *moved = ffn_backward(
                grad,
                resid,
                gains[layers + level][None],
                mixing[level],
                *w_ffn[level],
                b_in,
                both,
                more,
                outer,
                inner,
                3 if more else 6,
            )
            part_gains[layers + level] = part_gain[0]
            if more:
                pushed_attn[level + 1] = moved[0]
            before, kept = kept_attn[level]
            grad, part_gain, grad_attn, *pushed_ffn[level] = attn_backward(
                grad,
                before,
                gains[level][None],
                w_attn[level],
                tables,
                marks,
                spot,
                kept,
                [grad_in.reshape(dp, rows, -1), grad_down.reshape(dp, rows, -1)],
                outer,
                inner,
                1,
            )
            part_gains[level] = part_gain[0]
        stacked = jnp.pad(jnp.stack(part_gains), ((0, 8 - 2 * layers), (0, 0)))
        stacked = jnp.transpose(stacked.reshape(8, dp, rows), (1, 0, 2))
        pushed_attn[0], gain_parts = push(
            [grad_attn.reshape(dp, rows, -1), stacked], outer, inner, 7
        )

        gain_part = jnp.sum(gain_parts, axis=0)
        gain_sum = jnp.sum(
            gather(jnp.pad(gain_part, ((0, 0), (0, 128 - rows))), dp, 8)[0], axis=0
        )
        grad_gain_attn = gain_sum[:layers, :rows]
        grad_gain_ffn = gain_sum[layers : 2 * layers, :rows]

        kinds = experts + 1
        ups, downs, attns = [], [], []
        for level in range(layers):
            in_part, down_part = pushed_ffn[level]
            attn_part = pushed_attn[level]
            ups.append(
                jnp.concatenate(
                    [
                        jnp.stack(
                            [
                                in_part[k][:, m * slim : (m + 1) * slim]
                                for m in range(2 * kinds)
                            ]
                        )
                        for k in range(outer)
                    ],
                    axis=2,
                )
            )
            downs.append(
                jnp.concatenate(
                    [
                        jnp.stack(
                            [
                                jnp.transpose(down_part[k][:, m * slim : (m + 1) * slim])
                                for m in range(kinds)
                            ]
                        )
                        for k in range(outer)
                    ],
                    axis=1,
                )
            )
            attns.append(jnp.sum(attn_part.astype(F32), axis=0))
        up = jnp.stack(ups).astype(F32)
        down = jnp.stack(downs).astype(F32)
        attn = jnp.stack(attns)
        quarter = attn.shape[-1] // 4
        return (
            mixed,
            grad,
            grad_gain_attn,
            attn[:, :, :quarter],
            attn[:, :, quarter : 2 * quarter],
            attn[:, :, 2 * quarter : 3 * quarter],
            jnp.swapaxes(attn[:, :, 3 * quarter :], 1, 2),
            grad_gain_ffn,
            up[:, :experts],
            up[:, kinds : kinds + experts],
            down[:, :experts],
            up[:, experts],
            up[:, kinds + experts],
            down[:, experts],
        )

    return body


def solution(mesh):
    return jax.shard_map(
        make_body(mesh.shape["dp"]),
        mesh=mesh,
        in_specs=(
            P(("dp", "tensor"), None),
            P("dp", None),
            P("dp", None),
            P(None, "dp", None),
            P(None, "dp", None),
            P(("dp", "tensor"), None),
            P(None, "dp"),
            P(None, "dp", "tensor"),
            P(None, "dp", "tensor"),
            P(None, "dp", "tensor"),
            P(None, "tensor", "dp"),
            P(None, "dp"),
            P(None, None, "dp", "tensor"),
            P(None, None, "dp", "tensor"),
            P(None, None, "tensor", "dp"),
            P(None, "dp", "tensor"),
            P(None, "dp", "tensor"),
            P(None, "tensor", "dp"),
        ),
        out_specs=(
            P(("dp", "tensor"), None),
            P(("dp", "tensor"), None),
            P(None, "dp"),
            P(None, "dp", "tensor"),
            P(None, "dp", "tensor"),
            P(None, "dp", "tensor"),
            P(None, "tensor", "dp"),
            P(None, "dp"),
            P(None, None, "dp", "tensor"),
            P(None, None, "dp", "tensor"),
            P(None, None, "tensor", "dp"),
            P(None, "dp", "tensor"),
            P(None, "dp", "tensor"),
            P(None, "tensor", "dp"),
        ),
        check_vma=False,
    )
```

time: 835 us -> 545 us (0.65); the launches traced: 819 us -> 539 us
  matrix products: 112 us -> 0 us
  Pallas kernels: 595 us -> 490 us
  local copies, waits for them, and re-layouts: 58.3 us -> 23.5 us
  other arithmetic: 51.1 us -> 24 us
    dot_general x36 -> x0, matrix products: 112 us -> none  [the longest x8 42.5 us: dot(): return jnp.dot(left, right, preferred_element_type=F32)]
    pallas_call x2 -> x1, Pallas kernels: 119 us -> 19.7 us  [push(): pl.pallas_call(functools.partial(push_kernel, outer, inner, count), out_s...]
    pallas_call x2 -> x1, Pallas kernels: 123 us -> 24 us  [fetch(): pl.pallas_call(functools.partial(fetch_kernel, outer, inner, count), out_...]
    pallas_call x17 -> x9, Pallas kernels: 353 us -> 446 us  [the longest x2 135 us: ffn_forward(): pl.pallas_call(functools.partial(ffn_forward_kernel, outer, inner, kinds,...]
    unnamed x351 -> x191, local copies, waits for them, and re-layouts: 34.5 us -> 8.04 us
    convert_element_type x11 -> x5, other arithmetic: 21.4 us -> 4.82 us  [the longest x1 1.76 us: body(): state = tokens.astype(F32)]
    reduce_sum x13 -> x3, other arithmetic: 13.6 us -> 1.62 us  [the longest x1 0.81 us: body(): gain_part = jnp.sum(gain_parts, axis=0)]
where the time goes in v2:
time: 545 us; the launch traced here: 539 us
  Pallas kernels  490 us (90%)
  other arithmetic  24 us (4%)
  local copies, waits for them, and re-layouts  23.5 us (4%)
    pallas_call x2, Pallas kernels, ffn_forward(): pl.pallas_call(functools.partial(ffn_forward_kernel, outer, inner, kinds,...  135 us
    pallas_call x2, Pallas kernels, ffn_backward(): pl.pallas_call(functools.partial(ffn_backward_kernel, outer, inner, kinds...  126 us
    pallas_call x2, Pallas kernels, attn_backward(): pl.pallas_call(functools.partial(attn_backward_kernel, outer, inner, coun...  94.2 us
    pallas_call x2, Pallas kernels, attn_forward(): pl.pallas_call(functools.partial(attn_forward_kernel, outer, inner, count...  82.7 us
    pallas_call x1, Pallas kernels, fetch(): pl.pallas_call(functools.partial(fetch_kernel, outer, inner, count), out_...  24 us
    pallas_call x1, Pallas kernels, push(): pl.pallas_call(functools.partial(push_kernel, outer, inner, count), out_s...  19.7 us

profile of v2, /device:TPU:9, one launch (start us, length us, event | category | flops | bytes accessed | tf_op | source)
XLA Modules:
  0.0 539.4 jit_solution(9264950518491487870)
XLA Ops:
  0.7 1.8 convert_element_type.242.refs_0_.refs_1_
  2.4 0.7 convert.81
  3.1 0.7 convert.80
  3.8 0.7 select_reduce_fusion
  5.2 1.0 copy.75
  6.2 0.9 convert.84
  7.2 0.9 convert.83
  8.2 0.8 pad_maximum_fusion.5
  9.0 24.0 %fetch.1 = (f32[8,16,512]{2,1,0:T(8,128)}, bf16[8,96,768]{2,1,0:T(8,128)(2,1)}) custom-call(f32[1,16,512]{2,1,0:T(8,128)} %maximum_bitcast_fusion.4.refs_0_, bf16[1,96,768]{2,1,0:T(8,128)(2,1)} %get-tuple-element.369.refs_1_), custom_call_target="tpu_custom_call" | custom-call | tf_op jit(solution)/shard_map/fetch/pallas_call | solution.py:88
  33.1 0.8 slice_bitcast_fusion.48
  33.9 0.7 slice.1106.refs_1_.refs_2_
  34.9 1.0 multiply_cosine_fusion
  35.9 1.3 maximum_maximum_fusion.refs_3_.refs_4_
  37.9 1.6 stack.515.refs_4_.refs_5_
  42.2 0.6 copy-done.9
  43.0 1.1 pad_maximum_fusion.refs_6_
  45.3 0.9 pad_maximum_fusion.2.refs_7_
  46.2 41.3 %attn_forward.2 = (f32[128,768]{1,0:T(8,128)}, bf16[4,128,768]{2,1,0:T(8,128)(2,1)}, bf16[4,128,384]{2,1,0:T(8,128)(2,1)}, bf16[4,128,192]{2,1,0:T(8,128)(2,1)},...) custom-call(f32[128,768]{1,0:T(8,128)} %convert_element_type.242.ref, ...), custom_call_target="tpu_custom_call" | custom-call | tf_op jit(solution)/shard_map/attn_forward/pallas_call | solution.py:887
  87.5 0.7 slice.1183.refs_1_.refs_2_
  88.2 0.6 constant_dynamic-slice_fusion
  88.9 1.5 copy.87
  90.3 1.5 fusion.14
  91.8 66.8 %ffn_forward.2 = (f32[128,768]{1,0:T(8,128)}, bf16[4,4,128,768]{3,2,1,0:T(8,128)(2,1)}, bf16[4,2,256,1280]{3,2,1,0:T(8,128)(2,1)}, bf16[8,96,768]{2,1,0:T(8,128)(2,1)}) custom-call(f32[128,768]{1,0:T(8,128)} %get-tuple-element.62.refs_0_.refs_1_, f32[1,768]{1,0:T(1,128)} %slice.1183.refs_1_.refs_2_, f32[4,2,256,4]{3,2,1,0:T(8,128)} %bitcast.761, ...), custom_call_target="tpu_custom_call" | custom-call | tf_op jit(solution)/shard_map/ffn_forward/pallas_call | solution.py:606
  158.7 0.7 slice.1191.refs_1_.refs_2_
  159.6 1.1 pad_maximum_fusion.1.refs_6_
  160.7 0.9 pad_maximum_fusion.3.refs_7_
  161.6 41.4 %attn_forward.3 = (f32[128,768]{1,0:T(8,128)}, bf16[4,128,768]{2,1,0:T(8,128)(2,1)}, bf16[4,128,384]{2,1,0:T(8,128)(2,1)}, bf16[4,128,192]{2,1,0:T(8,128)(2,1)},...) custom-call(f32[128,768]{1,0:T(8,128)} %get-tuple-element.65.refs_0_, ...), custom_call_target="tpu_custom_call" | custom-call | tf_op jit(solution)/shard_map/attn_forward/pallas_call | solution.py:887
  203.0 0.7 slice.1268.refs_1_.refs_2_
  203.6 68.7 %ffn_forward.3 = (f32[128,768]{1,0:T(8,128)}, bf16[4,4,128,768]{3,2,1,0:T(8,128)(2,1)}, bf16[4,2,256,1280]{3,2,1,0:T(8,128)(2,1)}) custom-call(f32[128,768]{1,0:T(8,128)} %get-tuple-element.67.refs_0_.refs_1_, f32[1,768]{1,0:T(1,128)} %slice.1268.refs_1_.refs_2_, f32[4,2,256,4]{3,2,1,0:T(8,128)} %bitcast.759, bf16[768,1280]{1,0:T(8,128)(2,1)} %bitcast.766, ...), custom_call_target="tpu_custom_call" | custom-call | tf_op jit(solution)/shard_map/ffn_forward/pallas_call | solution.py:606
  272.3 1.7 convert_element_type.287
  274.0 0.8 convert_element_type.288.refs_0_
  274.8 62.8 %ffn_backward.2 = (f32[128,768]{1,0:T(8,128)}, f32[1,768]{1,0:T(1,128)}, bf16[768,1280]{1,0:T(8,128)(2,1)}, bf16[768,640]{1,0:T(8,128)(2,1)}) custom-call(f32[128,768]{1,0:T(8,128)} %convert_element_type.288.refs_0_, f32[128,768]{1,0:T(8,128)} %get-tuple-element.67.refs_0_.refs_1_, f32[1,768]{1,0:T(1,128)} %slice.1268.refs_1_.refs_2_, ...), custom_call_target="tpu_custom_call" | custom-call | tf_op jit(solution)/shard_map/ffn_backward/pallas_call | solution.py:746
  337.7 44.7 %attn_backward.2 = (f32[128,768]{1,0:T(8,128)}, f32[1,768]{1,0:T(1,128)}, bf16[768,768]{1,0:T(8,128)(2,1)}, bf16[4,96,1280]{2,1,0:T(8,128)(2,1)}, bf16[4,96,640]{2,1,0:T(8,128)(2,1)}) custom-call(f32[128,768]{1,0:T(8,128)} %get-tuple-element.73.refs_0_, f32[128,768]{1,0:T(8,128)} %get-tuple-element.65.refs_0_.refs_1_, f32[1,768]{1,0:T(1,128)} %slice.1191.refs_1_.refs_2_, ...), custom_call_target="tpu_custom_call" | custom-call | tf_op jit(solution)/shard_map/attn_backward/pallas_call | solution.py:1014
  382.3 63.2 %ffn_backward.3 = (f32[128,768]{1,0:T(8,128)}, f32[1,768]{1,0:T(1,128)}, bf16[768,1280]{1,0:T(8,128)(2,1)}, bf16[768,640]{1,0:T(8,128)(2,1)}, bf16[4,96,768]{2,1,0:T(8,128)(2,1)}) custom-call(f32[128,768]{1,0:T(8,128)} %get-tuple-element.81.refs_0_, f32[128,768]{1,0:T(8,128)} %get-tuple-element.62.refs_0_.refs_1_, f32[1,768]{1,0:T(1,128)} %slice.1183.refs_1_.refs_2_, ...), custom_call_target="tpu_custom_call" | custom-call | tf_op jit(solution)/shard_map/ffn_backward/pallas_call | solution.py:746
  445.6 49.5 %attn_backward.3 = (f32[128,768]{1,0:T(8,128)}, f32[1,768]{1,0:T(1,128)}, bf16[768,768]{1,0:T(8,128)(2,1)}, bf16[4,96,1280]{2,1,0:T(8,128)(2,1)}, bf16[4,96,640]{2,1,0:T(8,128)(2,1)}) custom-call(f32[128,768]{1,0:T(8,128)} %get-tuple-element.85.refs_0_, f32[128,768]{1,0:T(8,128)} %convert_element_type.242.refs_0_.refs_1_, f32[1,768]{1,0:T(1,128)} %slice.1106.refs_1_.refs_2_, ...), custom_call_target="tpu_custom_call" | custom-call | tf_op jit(solution)/shard_map/attn_backward/pallas_call | solution.py:1014
  495.2 0.7 select_maximum_fusion
  496.6 19.7 %push.1 = (bf16[4,96,768]{2,1,0:T(8,128)(2,1)}, f32[4,8,96]{2,1,0:T(8,128)}) custom-call(bf16[8,96,768]{2,1,0:T(8,128)(2,1)} %bitcast.778, f32[8,8,96]{2,1,0:T(8,128)} %bitcast.800), custom_call_target="tpu_custom_call" | custom-call | tf_op jit(solution)/shard_map/push/pallas_call | solution.py:111
  516.3 0.8 reduce_sum.62
  517.7 7.6 %gather.1 = f32[1,4,8,128]{3,2,1,0:T(8,128)} custom-call(f32[8,128]{1,0:T(8,128)} %pad.18.own), custom_call_target="tpu_custom_call" | custom-call | tf_op jit(solution)/shard_map/gather/pallas_call | solution.py:64
  525.3 0.7 reduce_sum.63
  526.7 1.2 convert_reduce_fusion.1
  527.9 0.9 fusion.3
  528.8 0.8 copy.89
  531.9 2.0 fusion.13
  535.4 1.3 slice.1710
  536.8 0.9 convert_bitcast_fusion.1
  537.7 0.8 convert_bitcast_fusion
  538.5 0.7 copy.301
  (258 shorter events, 11.1 us)
Async XLA Ops:
  0.6 7.5 %copy-start.14 = (f32[2,96,192]{2,1,0:T(8,128)S(1)}, f32[2,96,192]{2,1,0:T(8,128)}, u32[]{:S(2)}) copy-start(f32[2,96,192]{2,1,0:T(8,128)} %param.25) | copy-start | bytes 442372
  0.7 34.1 %copy-start.25 = (s32[1,512]{1,0:T(1,128)S(1)}, s32[1,512]{1,0:T(1,128)}, u32[]{:S(2)}) copy-start(s32[1,512]{1,0:T(1,128)} %param.19) | copy-start | bytes 6148
  0.7 33.9 %copy-start.29 = (s32[1,3]{1,0:T(1,128)S(1)}, s32[1,3]{1,0:T(1,128)}, u32[]{:S(2)}) copy-start(s32[1,3]{1,0:T(1,128)} %param.20) | copy-start | bytes 40
  37.4 2.7 copy-start
  40.2 1.0 copy-start.8
  40.2 1.6 copy-start.1
  40.7 0.7 copy-start.12
  41.9 1.0 copy-start.9
  42.0 2.0 copy-start.2
  44.1 1.0 copy-start.10
  44.6 0.7 copy-start.16
  44.6 0.7 copy-start.18
  44.6 0.7 copy-start.20
  44.6 0.7 copy-start.22
  46.2 42.0 %copy-start.24 = (f32[8,16,512]{2,1,0:T(8,128)S(1)}, f32[8,16,512]{2,1,0:T(8,128)}, u32[]{:S(2)}) copy-start(f32[8,16,512]{2,1,0:T(8,128)} %get-tuple-element.60) | copy-start | bytes 786436
  91.8 67.5 %copy-start.13 = (bf16[96,1280]{1,0:T(8,128)(2,1)S(1)}, bf16[96,1280]{1,0:T(8,128)(2,1)}, u32[]{:S(2)}) copy-start(bf16[96,1280]{1,0:T(8,128)(2,1)} %copy-done.12) | copy-start | bytes 737284
  158.6 2.0 copy-start.17
  158.6 2.0 copy-start.19
  158.6 2.0 copy-start.21
  158.6 2.0 copy-start.23
  203.6 70.4 %copy-start.15 = (bf16[128,768]{1,0:T(8,128)(2,1)S(1)}, bf16[128,768]{1,0:T(8,128)(2,1)}, u32[]{:S(2)}) copy-start(bf16[128,768]{1,0:T(8,128)(2,1)} %param.23) | copy-start | bytes 589828
  445.6 49.6 %copy-start.26 = (f32[1,768]{1,0:T(1,128)S(1)}, f32[1,768]{1,0:T(1,128)}, u32[]{:S(2)}) copy-start(f32[1,768]{1,0:T(1,128)} %get-tuple-element.98) | copy-start | bytes 9220
  445.6 49.6 %copy-start.27 = (f32[1,768]{1,0:T(1,128)S(1)}, f32[1,768]{1,0:T(1,128)}, u32[]{:S(2)}) copy-start(f32[1,768]{1,0:T(1,128)} %get-tuple-element.96) | copy-start | bytes 9220
  445.6 49.6 %copy-start.28 = (f32[1,768]{1,0:T(1,128)S(1)}, f32[1,768]{1,0:T(1,128)}, u32[]{:S(2)}) copy-start(f32[1,768]{1,0:T(1,128)} %get-tuple-element.97) | copy-start | bytes 9220
  445.6 81.0 %copy-start.5 = (bf16[4,96,768]{2,1,0:T(8,128)(2,1)S(1)}, bf16[4,96,768]{2,1,0:T(8,128)(2,1)}, u32[]{:S(2)}) copy-start(bf16[4,96,768]{2,1,0:T(8,128)(2,1)} %get-tuple-element.101) | copy-start | bytes 1769476
  516.3 13.3 %copy-start.4 = (bf16[4,96,1280]{2,1,0:T(8,128)(2,1)S(1)}, bf16[4,96,1280]{2,1,0:T(8,128)(2,1)}, u32[]{:S(2)}) copy-start(bf16[4,96,1280]{2,1,0:T(8,128)(2,1)} %get-tuple-element.103) | copy-start | bytes 2949124
  529.7 1.2 copy-start.3
  531.9 2.0 copy-start.7
  533.8 1.0 copy-start.6
  536.8 1.7 copy-start.11
